TPU v7x, 32 devices: a whole 2x2x4 slice. The times are simulated.
32 devices in a mesh: wide: 8 (over z, x), narrow: 4 (over y, core).
Axes of the slice: x: 2, y: 2, z: 4, core: 2. Of those that a mesh axis runs over, the one named last changes fastest.
Arguments:
- factors: bfloat16 [192, 256, 768], P(('wide', 'narrow')), may hold values from -0.21875 to 0.21875
- integrals: bfloat16 [192, 256, 768], P(('wide', 'narrow')), may hold values from -6 to 6
- pao_energy: float32 [192, 256], replicated, may hold values from 0.3 to 4
- lmo_energy: float32 [192], replicated, may hold values from -1.5 to -0.3
- partners: int32 [192, 4], replicated, may hold values from 0 to 191, as said below
Outputs:
- auxiliary_density: float32 [768, 768], P('wide', 'narrow')
Inputs may be any that keep to these rules, and one draw needn't show every extreme that they name: LMO i is held by device i // 6, devices counted with wide outermost. Each LMO's 4 partners are LMOs other than itself, held by devices with the same narrow index as its own holder, in 4 different wide groups (its own device may be one). The listed pairs of one device's 6 LMOs point to exactly 8 devices, with exactly 3 pairs and exactly 2 distinct partners on each of them.
All inputs are finite; a program needn't handle non-finite values.
Results may differ from a plain program's by a relative error of at most 0.0035.
Values may be sent and summed in bfloat16 or wider, within the bound.
No kernel may reach another device: no remote copies, remote signals or barrier semaphores. Data moves between devices by JAX's collectives and lax.ppermute only.
A program may use at most 128 MiB of HBM per device.

v0:
```python
import functools

import jax
import jax.numpy as jnp
from jax import lax
from jax.experimental import pallas as pl
from jax.experimental.pallas import tpu as pltpu
from jax.sharding import PartitionSpec as P


PARTNERS = 4
F32 = jnp.float32
BF16 = jnp.bfloat16
VMEM_LIMIT = 24 << 20


def xor_permute(x, axis, bit):
    return lax.ppermute(x, axis, [(i, i ^ bit) for i in range(lax.axis_size(axis))])


def take_kernel(base, rows, index_ref, source_ref, *refs):
    outputs, (buffer, loaded, stored) = refs[:-3], refs[-3:]
    first, count = rows
    loads, stores = [], []
    for k in range(2 * len(outputs)):
        lmo = source_ref.at[index_ref[base + k], pl.ds(first, count), :]
        loads.append(pltpu.make_async_copy(lmo, buffer.at[k], loaded.at[k]))
        target = outputs[k // 2].at[k % 2]
        stores.append(pltpu.make_async_copy(buffer.at[k], target, stored.at[k]))
    for load in loads:
        load.start()
    for load, store in zip(loads, stores):
        load.wait()
        store.start()
    for store in stores:
        store.wait()


def take_pairs(source, index, base, outputs, first, count):
    auxiliary = source.shape[2]
    any_spec = pl.BlockSpec(memory_space=pl.ANY)
    return pl.pallas_call(
        functools.partial(take_kernel, base, (first, count)),
        out_shape=[jax.ShapeDtypeStruct((2, count, auxiliary), source.dtype)] * outputs,
        grid_spec=pltpu.PrefetchScalarGridSpec(
            num_scalar_prefetch=1,
            grid=(1,),
            in_specs=[pl.BlockSpec(memory_space=pltpu.HBM)],
            out_specs=[any_spec] * outputs,
            scratch_shapes=[
                pltpu.VMEM((2 * outputs, count, auxiliary), source.dtype),
                pltpu.SemaphoreType.DMA((2 * outputs,)),
                pltpu.SemaphoreType.DMA((2 * outputs,)),
            ],
        ),
        cost_estimate=pl.CostEstimate(
            flops=0, transcendentals=0, bytes_accessed=8 * outputs * count * auxiliary
        ),
        compiler_params=pltpu.CompilerParams(vmem_limit_bytes=VMEM_LIMIT),
        name="take_pairs",
    )(index, source)


def start_all(copies):
    for copy in copies:
        copy.start()


def load_sets(sets, meta_ref, part_refs, buffers, sem):
    copies, part_refs = [], iter(part_refs)
    for (base, _, _, counts), buffer in zip(sets, buffers):
        loads, row = [], 0
        for count in counts:
            part_ref = next(part_refs)
            for r in range(2):
                slot = r if part_ref.shape[0] == 2 else meta_ref[base + r]
                target = buffer.at[r, pl.ds(row, count), :]
                number = sum(len(c) for c in copies) + len(loads)
                loads.append(pltpu.make_async_copy(part_ref.at[slot], target, sem.at[number]))
            row += count
        copies.append(loads)
    return copies


def add_sets(sets, copies, buffers, steps, meta_ref, energy_ref, factors_ref, density_ref):
    for (base, group, first, counts), loads, buffer in zip(sets, copies, buffers):
        for copy in loads:
            copy.wait()
        for k in range(steps):

            @pl.when(meta_ref[base + 2 + 3 * k] > 0)
            def _():
                lmo, rank = meta_ref[base + 3 + 3 * k], meta_ref[base + 4 + 3 * k]
                energy = energy_ref[group]
                own_energy = jnp.broadcast_to(energy[k : k + 1], (8, energy.shape[1])).T[:, :1]
                other = energy[steps + k : steps + k + 1, first : first + sum(counts)]
                part = buffer[rank]
                integral = lax.dot_general(
                    factors_ref[lmo], part, (((1,), (1,)), ((), ())), preferred_element_type=F32
                )
                amplitude = (integral / (own_energy + other)).astype(BF16)
                density_ref[lmo] += jnp.dot(amplitude, part, preferred_element_type=F32)


def pair_kernel(sets, steps, initial, meta_ref, energy_ref, factors_ref, *refs):
    count = sum(len(counts) for *_, counts in sets)
    part_refs, refs = refs[:count], refs[count if initial else count + 1 :]
    density_ref, buffers, sem = refs[0], refs[1:-1], refs[-1]
    copies = load_sets(sets, meta_ref, part_refs, buffers, sem)
    for loads in copies:
        start_all(loads)
    if initial:
        density_ref[...] = jnp.zeros_like(density_ref)
    add_sets(sets, copies, buffers, steps, meta_ref, energy_ref, factors_ref, density_ref)


def set_shapes(sets, steps):
    static = tuple(
        ((2 + 3 * steps) * group, group, first, tuple(part.shape[1] for part in parts))
        for group, parts, first in sets
    )
    return static, [part for _, parts, _ in sets for part in parts]


def set_scratch(static, auxiliary):
    count = sum(2 * len(counts) for *_, counts in static)
    return [
        pltpu.VMEM((2, sum(counts), auxiliary), BF16) for *_, counts in static
    ], pltpu.SemaphoreType.DMA((count,))


def pair_terms(meta, energy, factors, sets, density):
    lmo_dev, orbitals, auxiliary = factors.shape
    steps = lmo_dev // 2
    static, parts = set_shapes(sets, steps)
    initial = density is None
    buffers, sem = set_scratch(static, auxiliary)
    any_spec = pl.BlockSpec(memory_space=pl.ANY)
    vmem_spec = pl.BlockSpec(memory_space=pltpu.VMEM)
    return pl.pallas_call(
        functools.partial(pair_kernel, static, steps, initial),
        out_shape=pltpu.VMEM((lmo_dev, orbitals, auxiliary), F32),
        in_specs=[pl.BlockSpec(memory_space=pltpu.SMEM), vmem_spec, vmem_spec]
        + [any_spec] * len(parts)
        + ([] if initial else [vmem_spec]),
        out_specs=vmem_spec,
        scratch_shapes=buffers + [sem],
        input_output_aliases={} if initial else {3 + len(parts): 0},
        cost_estimate=pl.CostEstimate(
            flops=4 * len(sets) * steps * orbitals * orbitals * auxiliary,
            transcendentals=len(sets) * steps * orbitals * orbitals,
            bytes_accessed=4 * len(sets) * orbitals * auxiliary,
        ),
        compiler_params=pltpu.CompilerParams(vmem_limit_bytes=VMEM_LIMIT),
        name="pair_terms",
    )(meta, energy, factors, *parts, *([] if initial else [density]))


def finish_kernel(sets, steps, slab, meta_ref, parity_ref, energy_ref, factors_ref, *refs):
    count = sum(len(counts) for *_, counts in sets)
    part_refs, refs = refs[:count], refs[count:]
    _, integrals_ref, keep_ref, send_ref, density_ref = refs[:5]
    buffers, (integrals, total, sem, integrals_sem) = refs[5:-4], refs[-4:]
    lmo_dev = density_ref.shape[0]
    copies = load_sets(sets, meta_ref, part_refs, buffers, sem)
    loads = [
        pltpu.make_async_copy(integrals_ref.at[i], integrals.at[i], integrals_sem.at[i])
        for i in range(lmo_dev)
    ]
    for group in copies:
        start_all(group)
    start_all(loads)
    add_sets(sets, copies, buffers, steps, meta_ref, energy_ref, factors_ref, density_ref)
    for i in range(lmo_dev):
        loads[i].wait()
        term = lax.dot_general(
            integrals[i], density_ref[i].astype(BF16), (((0,), (0,)), ((), ())),
            preferred_element_type=F32,
        )
        if i == 0:
            total[...] = term
        else:
            total[...] += term
    value = total[...]
    total[...] = 0.5 * (value + value.T)
    parity = parity_ref[0]
    for q in range(keep_ref.shape[0]):
        keep_ref[q] = total[pl.ds((2 * q + parity) * slab, slab), :]
        send_ref[q] = total[pl.ds((2 * q + 1 - parity) * slab, slab), :].astype(BF16)


def finish(meta, parity, energy, factors, sets, density, integrals, narrow_count):
    lmo_dev, orbitals, auxiliary = density.shape
    steps = lmo_dev // 2
    static, parts = set_shapes(sets, steps)
    slab = auxiliary // narrow_count
    out = (narrow_count // 2, slab, auxiliary)
    buffers, sem = set_scratch(static, auxiliary)
    any_spec = pl.BlockSpec(memory_space=pl.ANY)
    vmem_spec = pl.BlockSpec(memory_space=pltpu.VMEM)
    smem_spec = pl.BlockSpec(memory_space=pltpu.SMEM)
    return pl.pallas_call(
        functools.partial(finish_kernel, static, steps, slab),
        out_shape=[
            pltpu.VMEM(out, F32),
            pltpu.VMEM(out, BF16),
            pltpu.VMEM(density.shape, F32),
        ],
        in_specs=[smem_spec, smem_spec, vmem_spec, vmem_spec]
        + [any_spec] * len(parts)
        + [vmem_spec, any_spec],
        out_specs=[vmem_spec] * 3,
        scratch_shapes=buffers
        + [
            pltpu.VMEM(integrals.shape, BF16),
            pltpu.VMEM((auxiliary, auxiliary), F32),
            sem,
            pltpu.SemaphoreType.DMA((lmo_dev,)),
        ],
        input_output_aliases={4 + len(parts): 2},
        cost_estimate=pl.CostEstimate(
            flops=2 * lmo_dev * orbitals * auxiliary * auxiliary,
            transcendentals=0,
            bytes_accessed=6 * density.size,
        ),
        compiler_params=pltpu.CompilerParams(vmem_limit_bytes=VMEM_LIMIT),
        name="finish",
    )(meta, parity, energy, factors, *parts, density, integrals)[:2]


def halve(x, axis, bit, high):
    pairs = x.reshape((x.shape[0] // 2, 2) + x.shape[1:])
    keep = jnp.where(high, pairs[:, 1], pairs[:, 0])
    send = jnp.where(high, pairs[:, 0], pairs[:, 1]).astype(BF16)
    return keep + xor_permute(send, axis, bit).astype(F32)


def bits_of(count):
    return [1 << b for b in range(count.bit_length() - 1)]


def local(factors, integrals, pao_energy, lmo_energy, partners):
    wide_count = lax.axis_size("wide")
    narrow_count = lax.axis_size("narrow")
    wide_index = lax.axis_index("wide")
    narrow_index = lax.axis_index("narrow")
    lmo_dev, orbitals, auxiliary = factors.shape
    pair_count = lmo_dev * PARTNERS
    group_pairs = lmo_dev // 2
    half = wide_count // 2
    chunk = orbitals * 5 // 16 // 16 * 16
    direct = 2 * chunk

    leading = factors[:, :chunk]
    leading, others = lax.optimization_barrier((leading, factors))
    mirrored = [xor_permute(x, "wide", half) for x in [leading, others[:, chunk:direct]]]

    column = lax.dynamic_index_in_dim(
        partners.reshape(wide_count, narrow_count, pair_count), narrow_index, 1, keepdims=False
    )
    groups = column // lmo_dev // narrow_count
    slots = column % lmo_dev
    ids = jnp.arange(wide_count, dtype=jnp.int32)
    hit = groups[:, :, None] == ids
    low = jnp.min(jnp.where(hit, slots[:, :, None], lmo_dev - 1), axis=1)
    high = jnp.max(jnp.where(hit, slots[:, :, None], 0), axis=1)
    asked = jnp.stack([low, high], axis=-1)
    order = wide_index ^ ids
    by_order = (order[:, None] == ids)[:, :, None]

    def asked_of(group):
        listed = lax.dynamic_index_in_dim(asked, group, 1, keepdims=False)
        return jnp.sum(jnp.where(by_order, listed[None], 0), axis=1, dtype=jnp.int32)

    asked = jnp.stack([asked_of(wide_index), asked_of(wide_index ^ half)]).reshape(-1)

    near = [
        xor_permute(x, "wide", d + 1)
        for d, x in enumerate(take_pairs(factors, asked, 2, half - 1, 0, orbitals))
    ]
    far_asked, mirrored[0] = lax.optimization_barrier((asked, mirrored[0]))
    far_rows = list(take_pairs(factors, far_asked, 2 * half, half, direct, orbitals - direct))
    late = half // 2
    forwarded = [
        [
            xor_permute(x, "wide", d + 1)
            for d, x in enumerate(take_pairs(m, asked, 2 * wide_count + 2, half - 1, 0, chunk))
        ]
        for m in mirrored
    ]

    far = []
    for d, x in enumerate(far_rows):
        if d >= late:
            x, far[d - late] = lax.optimization_barrier((x, far[d - late]))
        far.append(xor_permute(x, "wide", half + d))

    own_groups = lax.dynamic_index_in_dim(groups, wide_index, 0, keepdims=False)
    own_slots = lax.dynamic_index_in_dim(slots, wide_index, 0, keepdims=False)
    listed = lax.dynamic_index_in_dim(column, wide_index, 0, keepdims=False)
    own_low = lax.dynamic_index_in_dim(low, wide_index, 0, keepdims=False)
    own_high = lax.dynamic_index_in_dim(high, wide_index, 0, keepdims=False)
    pair_ids = jnp.arange(pair_count, dtype=jnp.int32)
    place = jnp.sum(
        (own_groups[:, None] == own_groups[None, :]) & (pair_ids[None, :] < pair_ids[:, None]),
        axis=1, dtype=jnp.int32,
    )
    steps = jnp.arange(group_pairs, dtype=jnp.int32)
    picked = (own_groups == order[:, None, None]) & (place == steps[None, :, None])

    def of_pair(values):
        return jnp.sum(jnp.where(picked, values, 0), axis=2, dtype=jnp.int32)

    valid = of_pair(jnp.ones_like(pair_ids))
    lmo = jnp.where(valid > 0, of_pair(pair_ids // PARTNERS), steps)
    lowest = jnp.sum(jnp.where(own_groups[:, None] == ids, own_low, 0), axis=1, dtype=jnp.int32)
    rank = of_pair((own_slots > lowest).astype(jnp.int32))
    bounds = jnp.stack([own_low, own_high], axis=-1)
    bounds = jnp.sum(jnp.where(by_order, bounds[None], 0), axis=1, dtype=jnp.int32)
    triples = jnp.stack([valid, lmo, rank], axis=-1).reshape(wide_count, 3 * group_pairs)
    meta = jnp.concatenate([bounds, triples], axis=1).reshape(-1)

    shifted = pao_energy - lmo_energy[:, None]
    first_lmo = (wide_index * narrow_count + narrow_index) * lmo_dev
    rows = jnp.concatenate([first_lmo + lmo, of_pair(listed)], axis=1)
    rows = jnp.pad(rows, ((0, 0), (0, -rows.shape[1] % 8)))
    energy = shifted.at[rows].get(mode="promise_in_bounds")

    highs = {("narrow", bit): (narrow_index & bit) > 0 for bit in bits_of(narrow_count)}
    highs |= {("wide", bit): (wide_index & bit) > 0 for bit in bits_of(wide_count)}
    parity = (narrow_index & 1).astype(jnp.int32).reshape(1)
    meta, parity, energy, highs = lax.optimization_barrier((meta, parity, energy, highs))

    def add(sets, density):
        return pair_terms(meta, energy, factors, sets, density)

    def far_set(d, begin, with_direct):
        parts = list(mirrored) if d == 0 else [pieces[d - 1] for pieces in forwarded]
        parts = parts[begin:] + [far[d]] if with_direct else parts[begin:1]
        return half + d, parts, begin * chunk

    density = add([(0, [factors], 0), (1, [near[0]], 0)], None)
    density = add([(d, [near[d - 1]], 0) for d in range(2, half)], density)
    density = add([far_set(d, 0, True) for d in range(late)], density)
    density = add([far_set(d, 0, False) for d in range(late, half)], density)

    keep, send = finish(
        meta, parity, energy, factors,
        [far_set(d, 1, True) for d in range(late, half)], density, integrals, narrow_count,
    )

    x = keep + xor_permute(send, "narrow", 1).astype(F32)
    for bit in bits_of(narrow_count)[1:]:
        x = halve(x, "narrow", bit, highs["narrow", bit])
    tile = (auxiliary // wide_count, auxiliary // narrow_count)
    x = x[0].T.reshape(wide_count, tile[0] * tile[1] // 128, 128)
    for bit in bits_of(wide_count):
        x = halve(x, "wide", bit, highs["wide", bit])
    return x[0].reshape(tile)


def solution(mesh):
    in_specs = (P(("wide", "narrow"), None, None), P(("wide", "narrow"), None, None), P(), P(), P())
    return jax.shard_map(
        local, mesh=mesh, in_specs=in_specs, out_specs=P("wide", "narrow"), check_vma=False
    )
```

profile of v0, /device:TPU:0, one launch (start us, length us, event | category | flops | bytes accessed | tf_op | source)
XLA Modules:
  0.0 182.5 jit_solution(1374585512167382883)
XLA Ops:
  4.0 3.2 %take_pairs.7 = (bf16[2,256,768]{2,1,0:T(8,128)(2,1)}, bf16[2,256,768]{2,1,0:T(8,128)(2,1)}, bf16[2,256,768]{2,1,0:T(8,128)(2,1)}) custom-call(s32[32]{0:T(128)S(1)} %reshape.298.index_ref, bf16[6,256,768]{2,1,0:T(8,128)(2,1)S(1)} %copy-done), custom_call_target="tpu_custom_call" | custom-call | bytes 4718592 | tf_op jit(solution)/shard_map/take_pairs/pallas_call | solution.py:42
  7.3 3.0 %collective-permute-start.14 = (bf16[2,256,768]{2,1,0:T(8,128)(2,1)}, bf16[2,256,768]{2,1,0:T(8,128)(2,1)}, u32[]{:S(2)}, u32[]{:S(2)}) collective-permute-start(bf16[2,256,768]{2,1,0:T(8,128)(2,1)} %get-tuple-element.62), channel_id=1, source_target_pairs={{0,4},{4,0},{8,12},{12,8},{16,20},{20,16},{24,28},{28,24},{1,5},{5... | collective-permute-start | bytes 2359304 | tf_op jit(solution)/shard_map/ppermute | solution.py:18
  12.8 3.0 %collective-permute-start.2 = (bf16[6,80,768]{2,1,0:T(8,128)(2,1)}, bf16[6,80,768]{2,1,0:T(8,128)(2,1)S(1)}, u32[]{:S(2)}, u32[]{:S(2)}) collective-permute-start(bf16[6,80,768]{2,1,0:T(8,128)(2,1)} %slice.38), channel_id=1, source_target_pairs={{0,16},{4,20},{8,24},{12,28},{16,0},{20,4},{24,8},{28,12},{1,17},{... | collective-permute-start | bytes 2211848 | tf_op jit(solution)/shard_map/ppermute | solution.py:18
  18.3 44.5 %collective-permute-done.2.source_ref.refs_0_ = bf16[6,80,768]{2,1,0:T(8,128)(2,1)S(1)} collective-permute-done((bf16[6,80,768]{2,1,0:T(8,128)(2,1)}, bf16[6,80,768]{2,1,0:T(8,128)(2,1)S(1)}, u32[]{:S(2)}, u32[]{:S(2)}) %collective-permute-start.2) | collective-permute-done | bytes 737312 | tf_op jit(solution)/shard_map/ppermute | solution.py:18
  62.8 3.4 %take_pairs.5 = (bf16[2,96,768]{2,1,0:T(8,128)(2,1)}, bf16[2,96,768]{2,1,0:T(8,128)(2,1)S(1)}, bf16[2,96,768]{2,1,0:T(8,128)(2,1)S(1)}, bf16[2,96,768]{2,1,0:T(8,128)(2,1)S(1)}) custom-call(s32[32]{0:T(128)S(1)} %reshape.298.index_ref, bf16[6,256,768]{2,1,0:T(8,128)(2,1)S(1)} %copy-done.1), custom_call_target="tpu_custom_call" | custom-call | bytes 2359296 | tf_op jit(solution)/shard_map/take_pairs/pallas_call | solution.py:42
  66.9 3.3 %collective-permute-start.6 = (bf16[2,96,768]{2,1,0:T(8,128)(2,1)S(1)}, bf16[2,96,768]{2,1,0:T(8,128)(2,1)S(1)}, u32[]{:S(2)}, u32[]{:S(2)}) collective-permute-start(bf16[2,96,768]{2,1,0:T(8,128)(2,1)S(1)} %get-tuple-element.51), channel_id=1, source_target_pairs={{0,20},{4,16},{8,28},{12,24},{16,4},{20,0},{24,12},{28,8},{1,21},{... | collective-permute-start | bytes 884744 | tf_op jit(solution)/shard_map/ppermute | solution.py:18
  70.2 8.4 %collective-permute-done.source_ref.refs_1_ = bf16[6,80,768]{2,1,0:T(8,128)(2,1)} collective-permute-done((bf16[6,80,768]{2,1,0:T(8,128)(2,1)}, bf16[6,80,768]{2,1,0:T(8,128)(2,1)}, u32[]{:S(2)}, u32[]{:S(2)}) %collective-permute-start) | collective-permute-done | bytes 737312 | tf_op jit(solution)/shard_map/ppermute | solution.py:18
  78.6 3.4 %collective-permute-start.3 = (bf16[2,96,768]{2,1,0:T(8,128)(2,1)}, bf16[2,96,768]{2,1,0:T(8,128)(2,1)}, u32[]{:S(2)}, u32[]{:S(2)}) collective-permute-start(bf16[2,96,768]{2,1,0:T(8,128)(2,1)} %get-tuple-element.47), channel_id=1, source_target_pairs={{0,16},{4,20},{8,24},{12,28},{16,0},{20,4},{24,8},{28,12},{1,17},{... | collective-permute-start | bytes 884744 | tf_op jit(solution)/shard_map/ppermute | solution.py:18
  82.1 2.4 %take_pairs.6 = (bf16[2,80,768]{2,1,0:T(8,128)(2,1)}, bf16[2,80,768]{2,1,0:T(8,128)(2,1)}, bf16[2,80,768]{2,1,0:T(8,128)(2,1)S(1)}) custom-call(s32[32]{0:T(128)S(1)} %reshape.298.index_ref, bf16[6,80,768]{2,1,0:T(8,128)(2,1)S(1)} %collective-permute-done.2.source_ref.refs_0_), custom_call_target="tpu_custom_call" | custom-call | bytes 1474560 | tf_op jit(solution)/shard_map/take_pairs/pallas_call | solution.py:42
  85.2 2.3 %take_pairs.4 = (bf16[2,80,768]{2,1,0:T(8,128)(2,1)}, bf16[2,80,768]{2,1,0:T(8,128)(2,1)S(1)}, bf16[2,80,768]{2,1,0:T(8,128)(2,1)S(1)}) custom-call(s32[32]{0:T(128)S(1)} %reshape.298.index_ref, bf16[6,80,768]{2,1,0:T(8,128)(2,1)} %collective-permute-done.source_ref.refs_1_), custom_call_target="tpu_custom_call" | custom-call | bytes 1474560 | tf_op jit(solution)/shard_map/take_pairs/pallas_call | solution.py:42
  88.9 5.0 %collective-permute-start.11 = (bf16[2,80,768]{2,1,0:T(8,128)(2,1)}, bf16[2,80,768]{2,1,0:T(8,128)(2,1)}, u32[]{:S(2)}, u32[]{:S(2)}) collective-permute-start(bf16[2,80,768]{2,1,0:T(8,128)(2,1)} %get-tuple-element.58), channel_id=1, source_target_pairs={{0,4},{4,0},{8,12},{12,8},{16,20},{20,16},{24,28},{28,24},{1,5},{5... | collective-permute-start | bytes 737288 | tf_op jit(solution)/shard_map/ppermute | solution.py:18
  96.0 10.4 %collective-permute-start.8 = (bf16[2,80,768]{2,1,0:T(8,128)(2,1)}, bf16[2,80,768]{2,1,0:T(8,128)(2,1)}, u32[]{:S(2)}, u32[]{:S(2)}) collective-permute-start(bf16[2,80,768]{2,1,0:T(8,128)(2,1)} %get-tuple-element.54), channel_id=1, source_target_pairs={{0,8},{4,12},{8,0},{12,4},{16,24},{20,28},{24,16},{28,20},{1,9},{5... | collective-permute-start | bytes 737288 | tf_op jit(solution)/shard_map/ppermute | solution.py:18
  109.8 5.3 %pair_terms.4.refs_2_ = f32[6,256,768]{2,1,0:T(8,128)S(1)} custom-call(s32[88]{0:T(128)S(1)} %reshape.296.meta_ref, f32[8,8,256]{2,1,0:T(8,128)S(1)} %bitcast.113, bf16[6,256,768]{2,1,0:T(8,128)(2,1)S(1)} %copy-done.1, bf16[6,256,768]{2,1,0:T(8,128)(2,1)S(1)} %copy-done.1, bf16[2,256,768]{2,1,0:T(8,128)(2,1)} %collective-permute-done.14.refs_1_), custom_call_target="tpu_custom_call" | custom-call | flops 1207959552 | bytes 1572864 | tf_op jit(solution)/shard_map/pair_terms/pallas_call | solution.py:140
  117.3 2.5 %collective-permute-start.7 = (bf16[2,96,768]{2,1,0:T(8,128)(2,1)S(1)}, bf16[2,96,768]{2,1,0:T(8,128)(2,1)S(1)}, u32[]{:S(2)}, u32[]{:S(2)}) collective-permute-start(bf16[2,96,768]{2,1,0:T(8,128)(2,1)S(1)} %copy-done.6), channel_id=1, source_target_pairs={{0,28},{4,24},{8,20},{12,16},{16,12},{20,8},{24,4},{28,0},{1,29},{... | collective-permute-start | bytes 884744 | tf_op jit(solution)/shard_map/ppermute | solution.py:18
  119.8 2.3 %collective-permute-start.4 = (bf16[2,96,768]{2,1,0:T(8,128)(2,1)S(1)}, bf16[2,96,768]{2,1,0:T(8,128)(2,1)S(1)}, u32[]{:S(2)}, u32[]{:S(2)}) collective-permute-start(bf16[2,96,768]{2,1,0:T(8,128)(2,1)S(1)} %copy-done.4), channel_id=1, source_target_pairs={{0,24},{4,28},{8,16},{12,20},{16,8},{20,12},{24,0},{28,4},{1,25},{... | collective-permute-start | bytes 884744 | tf_op jit(solution)/shard_map/ppermute | solution.py:18
  122.1 5.8 %pair_terms.5.refs_6_ = f32[6,256,768]{2,1,0:T(8,128)S(1)} custom-call(s32[88]{0:T(128)S(1)} %reshape.296.meta_ref, f32[8,8,256]{2,1,0:T(8,128)S(1)} %bitcast.114, bf16[6,256,768]{2,1,0:T(8,128)(2,1)S(1)} %copy-done.1, bf16[2,256,768]{2,1,0:T(8,128)(2,1)} %collective-permute-done.12.refs_0_, ...), custom_call_target="tpu_custom_call", output_to_operand_aliasing={{}: (5, {})} | custom-call | flops 1207959552 | bytes 1572864 | tf_op jit(solution)/shard_map/pair_terms/pallas_call | solution.py:140
  127.9 6.1 %pair_terms.6.refs_2_ = f32[6,256,768]{2,1,0:T(8,128)S(1)} custom-call(s32[88]{0:T(128)S(1)} %reshape.296.meta_ref, f32[8,8,256]{2,1,0:T(8,128)S(1)} %bitcast.115, bf16[6,256,768]{2,1,0:T(8,128)(2,1)S(1)} %copy-done.1, bf16[6,80,768]{2,1,0:T(8,128)(2,1)S(1)} %collective-permute-done.2.source_ref.refs_0_, ...), custom_call_target="tpu_custom_call", output_to_operand_aliasing={{}: (9, {})} | custom-call | flops 1207959552 | bytes 1572864 | tf_op jit(solution)/shard_map/pair_terms/pallas_call | solution.py:140
  134.0 5.5 %pair_terms.7.refs_4_ = f32[6,256,768]{2,1,0:T(8,128)S(1)} custom-call(s32[88]{0:T(128)S(1)} %reshape.296.meta_ref, f32[8,8,256]{2,1,0:T(8,128)S(1)} %bitcast.116, bf16[6,256,768]{2,1,0:T(8,128)(2,1)S(1)} %copy-done.1, bf16[2,80,768]{2,1,0:T(8,128)(2,1)} %collective-permute-done.8.refs_0_, ...), custom_call_target="tpu_custom_call", output_to_operand_aliasing={{}: (5, {})} | custom-call | flops 1207959552 | bytes 1572864 | tf_op jit(solution)/shard_map/pair_terms/pallas_call | solution.py:140
  140.3 11.1 %finish.1 = (f32[2,192,768]{2,1,0:T(8,128)S(1)}, bf16[2,192,768]{2,1,0:T(8,128)(2,1)S(1)}, f32[6,256,768]{2,1,0:T(8,128)S(1)}) custom-call(s32[88]{0:T(128)S(1)} %reshape.296.meta_ref, s32[1]{0:T(128)} %bitcast.13.parity_ref, f32[8,8,256]{2,1,0:T(8,128)S(1)} %bitcast.117, bf16[6,256,768]{2,1,0:T(8,128)(2,1)S(1)} %copy-done.1, ...), custom_call_target="tpu_custom_call", output_to_operand_aliasing={{2}: (8, {})} | custom-call | flops 1811939328 | bytes 7077888 | tf_op jit(solution)/shard_map/finish/pallas_call | solution.py:202
  155.3 7.5 %collective-permute-done.16 = bf16[1,192,768]{2,1,0:T(8,128)(2,1)S(1)} collective-permute-done((bf16[1,192,768]{2,1,0:T(8,128)(2,1)S(1)}, bf16[1,192,768]{2,1,0:T(8,128)(2,1)S(1)}, u32[]{:S(2)}, u32[]{:S(2)}) %collective-permute-start.16) | collective-permute-done | bytes 294944 | tf_op jit(solution)/shard_map/ppermute | solution.py:18
  164.2 4.6 %collective-permute-done.17 = bf16[4,144,128]{2,1,0:T(8,128)(2,1)S(1)} collective-permute-done((bf16[4,144,128]{2,1,0:T(8,128)(2,1)S(1)}, bf16[4,144,128]{2,1,0:T(8,128)(2,1)S(1)}, u32[]{:S(2)}, u32[]{:S(2)}) %collective-permute-start.17) | collective-permute-done | bytes 147488 | tf_op jit(solution)/shard_map/ppermute | solution.py:18
  168.9 5.6 %collective-permute-start.18 = (bf16[2,144,128]{2,1,0:T(8,128)(2,1)S(1)}, bf16[2,144,128]{2,1,0:T(8,128)(2,1)S(1)}, u32[]{:S(2)}, u32[]{:S(2)}) collective-permute-start(bf16[2,144,128]{2,1,0:T(8,128)(2,1)S(1)} %fusion.8), channel_id=1, source_target_pairs={{0,8},{4,12},{8,0},{12,4},{16,24},{20,28},{24,16},{28,20},{1,9},{5... | collective-permute-start | bytes 221192 | tf_op jit(solution)/shard_map/ppermute | solution.py:18
  174.5 2.3 %collective-permute-done.18 = bf16[2,144,128]{2,1,0:T(8,128)(2,1)S(1)} collective-permute-done((bf16[2,144,128]{2,1,0:T(8,128)(2,1)S(1)}, bf16[2,144,128]{2,1,0:T(8,128)(2,1)S(1)}, u32[]{:S(2)}, u32[]{:S(2)}) %collective-permute-start.18) | collective-permute-done | bytes 73760 | tf_op jit(solution)/shard_map/ppermute | solution.py:18
  178.0 3.8 %collective-permute-done.19 = bf16[1,144,128]{2,1,0:T(8,128)(2,1)S(1)} collective-permute-done((bf16[1,144,128]{2,1,0:T(8,128)(2,1)S(1)}, bf16[1,144,128]{2,1,0:T(8,128)(2,1)S(1)}, u32[]{:S(2)}, u32[]{:S(2)}) %collective-permute-start.19) | collective-permute-done | bytes 36896 | tf_op jit(solution)/shard_map/ppermute | solution.py:18
  (106 shorter events, 27.3 us)
Async XLA Ops:
  4.0 13.5 %copy-start.12 = (f32[192,256]{1,0:T(8,128)S(1)}, f32[192,256]{1,0:T(8,128)}, u32[]{:S(2)}) copy-start(f32[192,256]{1,0:T(8,128)} %param.7) | copy-start | bytes 589828
  4.0 13.5 %copy-start.13 = (f32[192]{0:T(256)S(1)}, f32[192]{0:T(256)}, u32[]{:S(2)}) copy-start(f32[192]{0:T(256)} %param.8) | copy-start | bytes 2308
  4.0 58.8 %copy-start.1 = (bf16[6,256,768]{2,1,0:T(8,128)(2,1)S(1)}, bf16[6,256,768]{2,1,0:T(8,128)(2,1)}, u32[]{:S(2)}) copy-start(bf16[6,256,768]{2,1,0:T(8,128)(2,1)} %factors_ref.9) | copy-start | bytes 7077892
  7.3 81.6 %collective-permute-start.14 = (bf16[2,256,768]{2,1,0:T(8,128)(2,1)}, bf16[2,256,768]{2,1,0:T(8,128)(2,1)}, u32[]{:S(2)}, u32[]{:S(2)}) collective-permute-start(bf16[2,256,768]{2,1,0:T(8,128)(2,1)} %get-tuple-element.62), channel_id=1, source_target_pairs={{0,4},{4,0},{8,12},{12,8},{16,20},{20,16},{24,28},{28,24},{1,5},{5... | collective-permute-start | bytes 2359304 | tf_op jit(solution)/shard_map/ppermute | solution.py:18
  10.3 83.6 %collective-permute-start.12 = (bf16[2,256,768]{2,1,0:T(8,128)(2,1)}, bf16[2,256,768]{2,1,0:T(8,128)(2,1)}, u32[]{:S(2)}, u32[]{:S(2)}) collective-permute-start(bf16[2,256,768]{2,1,0:T(8,128)(2,1)} %get-tuple-element.60), channel_id=1, source_target_pairs={{0,8},{4,12},{8,0},{12,4},{16,24},{20,28},{24,16},{28,20},{1,9},{5... | collective-permute-start | bytes 2359304 | tf_op jit(solution)/shard_map/ppermute | solution.py:18
  11.9 103.3 %collective-permute-start.13 = (bf16[2,256,768]{2,1,0:T(8,128)(2,1)}, bf16[2,256,768]{2,1,0:T(8,128)(2,1)}, u32[]{:S(2)}, u32[]{:S(2)}) collective-permute-start(bf16[2,256,768]{2,1,0:T(8,128)(2,1)} %get-tuple-element.61), channel_id=1, source_target_pairs={{0,12},{4,8},{8,4},{12,0},{16,28},{20,24},{24,20},{28,16},{1,13},{... | collective-permute-start | bytes 2359304 | tf_op jit(solution)/shard_map/ppermute | solution.py:18
  12.8 50.0 %collective-permute-start.2 = (bf16[6,80,768]{2,1,0:T(8,128)(2,1)}, bf16[6,80,768]{2,1,0:T(8,128)(2,1)S(1)}, u32[]{:S(2)}, u32[]{:S(2)}) collective-permute-start(bf16[6,80,768]{2,1,0:T(8,128)(2,1)} %slice.38), channel_id=1, source_target_pairs={{0,16},{4,20},{8,24},{12,28},{16,0},{20,4},{24,8},{28,12},{1,17},{... | collective-permute-start | bytes 2211848 | tf_op jit(solution)/shard_map/ppermute | solution.py:18
  16.7 61.9 %collective-permute-start = (bf16[6,80,768]{2,1,0:T(8,128)(2,1)}, bf16[6,80,768]{2,1,0:T(8,128)(2,1)}, u32[]{:S(2)}, u32[]{:S(2)}) collective-permute-start(bf16[6,80,768]{2,1,0:T(8,128)(2,1)} %slice.39), channel_id=1, source_target_pairs={{0,16},{4,20},{8,24},{12,28},{16,0},{20,4},{24,8},{28,12},{1,17},{... | collective-permute-start | bytes 2211848 | tf_op jit(solution)/shard_map/ppermute | solution.py:18
  66.9 29.1 %copy-start.3 = (bf16[2,96,768]{2,1,0:T(8,128)(2,1)}, bf16[2,96,768]{2,1,0:T(8,128)(2,1)S(1)}, u32[]{:S(2)}) copy-start(bf16[2,96,768]{2,1,0:T(8,128)(2,1)S(1)} %get-tuple-element.48) | copy-start | bytes 884740
  66.9 29.1 %collective-permute-start.6 = (bf16[2,96,768]{2,1,0:T(8,128)(2,1)S(1)}, bf16[2,96,768]{2,1,0:T(8,128)(2,1)S(1)}, u32[]{:S(2)}, u32[]{:S(2)}) collective-permute-start(bf16[2,96,768]{2,1,0:T(8,128)(2,1)S(1)} %get-tuple-element.51), channel_id=1, source_target_pairs={{0,20},{4,16},{8,28},{12,24},{16,4},{20,0},{24,12},{28,8},{1,21},{... | collective-permute-start | bytes 884744 | tf_op jit(solution)/shard_map/ppermute | solution.py:18
  78.6 29.7 %collective-permute-start.3 = (bf16[2,96,768]{2,1,0:T(8,128)(2,1)}, bf16[2,96,768]{2,1,0:T(8,128)(2,1)}, u32[]{:S(2)}, u32[]{:S(2)}) collective-permute-start(bf16[2,96,768]{2,1,0:T(8,128)(2,1)} %get-tuple-element.47), channel_id=1, source_target_pairs={{0,16},{4,20},{8,24},{12,28},{16,0},{20,4},{24,8},{28,12},{1,17},{... | collective-permute-start | bytes 884744 | tf_op jit(solution)/shard_map/ppermute | solution.py:18
  88.9 28.4 %collective-permute-start.11 = (bf16[2,80,768]{2,1,0:T(8,128)(2,1)}, bf16[2,80,768]{2,1,0:T(8,128)(2,1)}, u32[]{:S(2)}, u32[]{:S(2)}) collective-permute-start(bf16[2,80,768]{2,1,0:T(8,128)(2,1)} %get-tuple-element.58), channel_id=1, source_target_pairs={{0,4},{4,0},{8,12},{12,8},{16,20},{20,16},{24,28},{28,24},{1,5},{5... | collective-permute-start | bytes 737288 | tf_op jit(solution)/shard_map/ppermute | solution.py:18
  93.9 23.4 %collective-permute-start.10 = (bf16[2,80,768]{2,1,0:T(8,128)(2,1)}, bf16[2,80,768]{2,1,0:T(8,128)(2,1)}, u32[]{:S(2)}, u32[]{:S(2)}) collective-permute-start(bf16[2,80,768]{2,1,0:T(8,128)(2,1)} %get-tuple-element.57), channel_id=1, source_target_pairs={{0,4},{4,0},{8,12},{12,8},{16,20},{20,16},{24,28},{28,24},{1,5},{5... | collective-permute-start | bytes 737288 | tf_op jit(solution)/shard_map/ppermute | solution.py:18
  96.0 23.8 %collective-permute-start.8 = (bf16[2,80,768]{2,1,0:T(8,128)(2,1)}, bf16[2,80,768]{2,1,0:T(8,128)(2,1)}, u32[]{:S(2)}, u32[]{:S(2)}) collective-permute-start(bf16[2,80,768]{2,1,0:T(8,128)(2,1)} %get-tuple-element.54), channel_id=1, source_target_pairs={{0,8},{4,12},{8,0},{12,4},{16,24},{20,28},{24,16},{28,20},{1,9},{5... | collective-permute-start | bytes 737288 | tf_op jit(solution)/shard_map/ppermute | solution.py:18
  108.3 25.7 %collective-permute-start.9 = (bf16[2,80,768]{2,1,0:T(8,128)(2,1)}, bf16[2,80,768]{2,1,0:T(8,128)(2,1)S(1)}, u32[]{:S(2)}, u32[]{:S(2)}) collective-permute-start(bf16[2,80,768]{2,1,0:T(8,128)(2,1)} %copy-done.11), channel_id=1, source_target_pairs={{0,12},{4,8},{8,4},{12,0},{16,28},{20,24},{24,20},{28,16},{1,13},{... | collective-permute-start | bytes 737288 | tf_op jit(solution)/shard_map/ppermute | solution.py:18
  115.2 24.4 %collective-permute-start.1 = (bf16[2,80,768]{2,1,0:T(8,128)(2,1)S(1)}, bf16[2,80,768]{2,1,0:T(8,128)(2,1)S(1)}, u32[]{:S(2)}, u32[]{:S(2)}) collective-permute-start(bf16[2,80,768]{2,1,0:T(8,128)(2,1)S(1)} %copy-done.10), channel_id=1, source_target_pairs={{0,8},{4,12},{8,0},{12,4},{16,24},{20,28},{24,16},{28,20},{1,9},{5... | collective-permute-start | bytes 737288 | tf_op jit(solution)/shard_map/ppermute | solution.py:18
  117.3 23.0 %collective-permute-start.5 = (bf16[2,80,768]{2,1,0:T(8,128)(2,1)S(1)}, bf16[2,80,768]{2,1,0:T(8,128)(2,1)S(1)}, u32[]{:S(2)}, u32[]{:S(2)}) collective-permute-start(bf16[2,80,768]{2,1,0:T(8,128)(2,1)S(1)} %copy-done.8), channel_id=1, source_target_pairs={{0,12},{4,8},{8,4},{12,0},{16,28},{20,24},{24,20},{28,16},{1,13},{... | collective-permute-start | bytes 737288 | tf_op jit(solution)/shard_map/ppermute | solution.py:18
  117.3 23.0 %collective-permute-start.7 = (bf16[2,96,768]{2,1,0:T(8,128)(2,1)S(1)}, bf16[2,96,768]{2,1,0:T(8,128)(2,1)S(1)}, u32[]{:S(2)}, u32[]{:S(2)}) collective-permute-start(bf16[2,96,768]{2,1,0:T(8,128)(2,1)S(1)} %copy-done.6), channel_id=1, source_target_pairs={{0,28},{4,24},{8,20},{12,16},{16,12},{20,8},{24,4},{28,0},{1,29},{... | collective-permute-start | bytes 884744 | tf_op jit(solution)/shard_map/ppermute | solution.py:18
  119.8 20.5 %collective-permute-start.4 = (bf16[2,96,768]{2,1,0:T(8,128)(2,1)S(1)}, bf16[2,96,768]{2,1,0:T(8,128)(2,1)S(1)}, u32[]{:S(2)}, u32[]{:S(2)}) collective-permute-start(bf16[2,96,768]{2,1,0:T(8,128)(2,1)S(1)} %copy-done.4), channel_id=1, source_target_pairs={{0,24},{4,28},{8,16},{12,20},{16,8},{20,12},{24,0},{28,4},{1,25},{... | collective-permute-start | bytes 884744 | tf_op jit(solution)/shard_map/ppermute | solution.py:18
  151.4 2.1 %collective-permute-start.15 = (bf16[2,192,768]{2,1,0:T(8,128)(2,1)S(1)}, bf16[2,192,768]{2,1,0:T(8,128)(2,1)S(1)}, u32[]{:S(2)}, u32[]{:S(2)}) collective-permute-start(bf16[2,192,768]{2,1,0:T(8,128)(2,1)S(1)} %get-tuple-element.64), channel_id=1, source_target_pairs={{0,1},{1,0},{2,3},{3,2},{4,5},{5,4},{6,7},{7,6},{8,9},{9,8},{10,11... | collective-permute-start | bytes 1769480 | tf_op jit(solution)/shard_map/ppermute | solution.py:18
  153.7 9.1 %collective-permute-start.16 = (bf16[1,192,768]{2,1,0:T(8,128)(2,1)S(1)}, bf16[1,192,768]{2,1,0:T(8,128)(2,1)S(1)}, u32[]{:S(2)}, u32[]{:S(2)}) collective-permute-start(bf16[1,192,768]{2,1,0:T(8,128)(2,1)S(1)} %fusion.1), channel_id=1, source_target_pairs={{0,2},{1,3},{2,0},{3,1},{4,6},{5,7},{6,4},{7,5},{8,10},{9,11},{10,... | collective-permute-start | bytes 884744 | tf_op jit(solution)/shard_map/ppermute | solution.py:18
  163.6 5.2 %collective-permute-start.17 = (bf16[4,144,128]{2,1,0:T(8,128)(2,1)S(1)}, bf16[4,144,128]{2,1,0:T(8,128)(2,1)S(1)}, u32[]{:S(2)}, u32[]{:S(2)}) collective-permute-start(bf16[4,144,128]{2,1,0:T(8,128)(2,1)S(1)} %fusion.4), channel_id=1, source_target_pairs={{0,4},{4,0},{8,12},{12,8},{16,20},{20,16},{24,28},{28,24},{1,5},{5... | collective-permute-start | bytes 442376 | tf_op jit(solution)/shard_map/ppermute | solution.py:18
  168.9 7.9 %collective-permute-start.18 = (bf16[2,144,128]{2,1,0:T(8,128)(2,1)S(1)}, bf16[2,144,128]{2,1,0:T(8,128)(2,1)S(1)}, u32[]{:S(2)}, u32[]{:S(2)}) collective-permute-start(bf16[2,144,128]{2,1,0:T(8,128)(2,1)S(1)} %fusion.8), channel_id=1, source_target_pairs={{0,8},{4,12},{8,0},{12,4},{16,24},{20,28},{24,16},{28,20},{1,9},{5... | collective-permute-start | bytes 221192 | tf_op jit(solution)/shard_map/ppermute | solution.py:18
  176.8 4.9 %collective-permute-start.19 = (bf16[1,144,128]{2,1,0:T(8,128)(2,1)S(1)}, bf16[1,144,128]{2,1,0:T(8,128)(2,1)S(1)}, u32[]{:S(2)}, u32[]{:S(2)}) collective-permute-start(bf16[1,144,128]{2,1,0:T(8,128)(2,1)S(1)} %fusion.9), channel_id=1, source_target_pairs={{0,16},{4,20},{8,24},{12,28},{16,0},{20,4},{24,8},{28,12},{1,17},{... | collective-permute-start | bytes 110600 | tf_op jit(solution)/shard_map/ppermute | solution.py:18
  (10 other events, 47.0 us)
where the time goes:
time: 183 us
  waiting for transfers between devices  75.9 us (41%)
  starting transfers between devices  47.2 us (26%)
  Pallas kernels  45.1 us (25%)
  local copies, waits for them, and re-layouts  10.8 us (6%)
  other arithmetic  3.09 us (2%)
    ppermute x20, waiting for transfers between devices, xor_permute(): lax.ppermute(x, axis, [(i, i ^ bit) for i in range(lax.axis_size(axis))])  75.9 us
    ppermute x20, starting transfers between devices, xor_permute(): lax.ppermute(x, axis, [(i, i ^ bit) for i in range(lax.axis_size(axis))])  47.2 us
    pallas_call x4, Pallas kernels, pair_terms(): pl.pallas_call(functools.partial(pair_kernel, static, steps, initial), ou...  22.7 us
    pallas_call x4, Pallas kernels, take_pairs(): pl.pallas_call(functools.partial(take_kernel, base, (first, count)), out_...  11.3 us
    pallas_call x1, Pallas kernels, finish(): pl.pallas_call(functools.partial(finish_kernel, static, steps, slab), out...  11.1 us
    unnamed x29, local copies, waits for them, and re-layouts  5.3 us
  transfers between devices with their start and end apart: 20, of which 9 were waited for; matrix products, arithmetic and copies ran while one was open for 3% of the time, Pallas kernels for 17%

commit v1 on v0

--- a/solution.py
+++ b/solution.py
@@ -12,6 +12,7 @@
 F32 = jnp.float32
 BF16 = jnp.bfloat16
 VMEM_LIMIT = 24 << 20
+MIRRORED_ROWS = (64, 144)
 
 
 def xor_permute(x, axis, bit):
@@ -156,25 +157,43 @@
     )(meta, energy, factors, *parts, *([] if initial else [density]))
 
 
+def dense_tiles(total, first, wide_count):
+    rows = total.shape[0] // wide_count
+    whole_even, middle, whole_odd = [
+        total[:, first + 128 * j : first + 128 * (j + 1)].reshape(wide_count, rows, 128)
+        for j in range(3)
+    ]
+    upper, lower = middle[:, : rows // 2], middle[:, rows // 2 :]
+    left = lax.broadcasted_iota(jnp.int32, upper.shape, 2) < 64
+    half_even = jnp.where(left, upper, pltpu.roll(lower, 64, axis=2))
+    half_odd = jnp.where(left, pltpu.roll(upper, 64, axis=2), lower)
+    return (
+        jnp.concatenate([whole_even, half_even], axis=1),
+        jnp.concatenate([whole_odd, half_odd], axis=1),
+    )
+
+
+def sparse_tile(dense, odd):
+    rows = dense.shape[0] * 2 // 3
+    whole = dense[:rows]
+    half = jnp.concatenate([dense[rows:, :64], dense[rows:, 64:]], axis=0)
+    return jnp.where(
+        odd, jnp.concatenate([half, whole], axis=1), jnp.concatenate([whole, half], axis=1)
+    )
+
+
 def finish_kernel(sets, steps, slab, meta_ref, parity_ref, energy_ref, factors_ref, *refs):
     count = sum(len(counts) for *_, counts in sets)
     part_refs, refs = refs[:count], refs[count:]
     _, integrals_ref, keep_ref, send_ref, density_ref = refs[:5]
-    buffers, (integrals, total, sem, integrals_sem) = refs[5:-4], refs[-4:]
-    lmo_dev = density_ref.shape[0]
+    buffers, (total, sem) = refs[5:-2], refs[-2:]
     copies = load_sets(sets, meta_ref, part_refs, buffers, sem)
-    loads = [
-        pltpu.make_async_copy(integrals_ref.at[i], integrals.at[i], integrals_sem.at[i])
-        for i in range(lmo_dev)
-    ]
     for group in copies:
         start_all(group)
-    start_all(loads)
     add_sets(sets, copies, buffers, steps, meta_ref, energy_ref, factors_ref, density_ref)
-    for i in range(lmo_dev):
-        loads[i].wait()
+    for i in range(density_ref.shape[0]):
         term = lax.dot_general(
-            integrals[i], density_ref[i].astype(BF16), (((0,), (0,)), ((), ())),
+            integrals_ref[i], density_ref[i].astype(BF16), (((0,), (0,)), ((), ())),
             preferred_element_type=F32,
         )
         if i == 0:
@@ -185,18 +204,33 @@
     total[...] = 0.5 * (value + value.T)
     parity = parity_ref[0]
     for q in range(keep_ref.shape[0]):
-        keep_ref[q] = total[pl.ds((2 * q + parity) * slab, slab), :]
-        send_ref[q] = total[pl.ds((2 * q + 1 - parity) * slab, slab), :].astype(BF16)
-
-
-def finish(meta, parity, energy, factors, sets, density, integrals, narrow_count):
+        if keep_ref.ndim == 3:
+            keep_ref[q] = total[pl.ds((2 * q + parity) * slab, slab), :]
+            send_ref[q] = total[pl.ds((2 * q + 1 - parity) * slab, slab), :].astype(BF16)
+            continue
+        even, odd = dense_tiles(total, 2 * q * slab, keep_ref.shape[1])
+
+        @pl.when(parity == 0)
+        def _():
+            keep_ref[q] = even
+            send_ref[q] = odd.astype(BF16)
+
+        @pl.when(parity == 1)
+        def _():
+            keep_ref[q] = odd
+            send_ref[q] = even.astype(BF16)
+
+
+def finish(meta, parity, energy, factors, sets, density, integrals, counts):
     lmo_dev, orbitals, auxiliary = density.shape
     steps = lmo_dev // 2
     static, parts = set_shapes(sets, steps)
-    slab = auxiliary // narrow_count
+    wide_count, narrow_count = counts
+    slab, rows = auxiliary // narrow_count, auxiliary // wide_count
     out = (narrow_count // 2, slab, auxiliary)
+    if slab == 192 and rows % 32 == 0:
+        out = (narrow_count // 2, wide_count, rows * slab // 128, 128)
     buffers, sem = set_scratch(static, auxiliary)
-    any_spec = pl.BlockSpec(memory_space=pl.ANY)
     vmem_spec = pl.BlockSpec(memory_space=pltpu.VMEM)
     smem_spec = pl.BlockSpec(memory_space=pltpu.SMEM)
     return pl.pallas_call(
@@ -207,16 +241,10 @@
             pltpu.VMEM(density.shape, F32),
         ],
         in_specs=[smem_spec, smem_spec, vmem_spec, vmem_spec]
-        + [any_spec] * len(parts)
-        + [vmem_spec, any_spec],
+        + [vmem_spec] * len(parts)
+        + [vmem_spec, vmem_spec],
         out_specs=[vmem_spec] * 3,
-        scratch_shapes=buffers
-        + [
-            pltpu.VMEM(integrals.shape, BF16),
-            pltpu.VMEM((auxiliary, auxiliary), F32),
-            sem,
-            pltpu.SemaphoreType.DMA((lmo_dev,)),
-        ],
+        scratch_shapes=buffers + [pltpu.VMEM((auxiliary, auxiliary), F32), sem],
         input_output_aliases={4 + len(parts): 2},
         cost_estimate=pl.CostEstimate(
             flops=2 * lmo_dev * orbitals * auxiliary * auxiliary,
@@ -228,10 +256,11 @@
     )(meta, parity, energy, factors, *parts, density, integrals)[:2]
 
 
-def halve(x, axis, bit, high):
-    pairs = x.reshape((x.shape[0] // 2, 2) + x.shape[1:])
-    keep = jnp.where(high, pairs[:, 1], pairs[:, 0])
-    send = jnp.where(high, pairs[:, 0], pairs[:, 1]).astype(BF16)
+def halve(x, axis, bit, high, dim):
+    pairs = x.reshape(x.shape[:dim] + (x.shape[dim] // 2, 2) + x.shape[dim + 1 :])
+    first, second = [lax.index_in_dim(pairs, b, dim + 1, keepdims=False) for b in range(2)]
+    keep = jnp.where(high, second, first)
+    send = jnp.where(high, first, second).astype(BF16)
     return keep + xor_permute(send, axis, bit).astype(F32)
 
 
@@ -248,8 +277,7 @@
     pair_count = lmo_dev * PARTNERS
     group_pairs = lmo_dev // 2
     half = wide_count // 2
-    chunk = orbitals * 5 // 16 // 16 * 16
-    direct = 2 * chunk
+    chunk, direct = [orbitals * c // 256 // 16 * 16 for c in MIRRORED_ROWS]
 
     leading = factors[:, :chunk]
     leading, others = lax.optimization_barrier((leading, factors))
@@ -284,16 +312,12 @@
     forwarded = [
         [
             xor_permute(x, "wide", d + 1)
-            for d, x in enumerate(take_pairs(m, asked, 2 * wide_count + 2, half - 1, 0, chunk))
+            for d, x in enumerate(take_pairs(m, asked, 2 * wide_count + 2, half - 1, 0, m.shape[1]))
         ]
         for m in mirrored
     ]
 
-    far = []
-    for d, x in enumerate(far_rows):
-        if d >= late:
-            x, far[d - late] = lax.optimization_barrier((x, far[d - late]))
-        far.append(xor_permute(x, "wide", half + d))
+    far = [xor_permute(x, "wide", half + d) for d, x in enumerate(far_rows)]
 
     own_groups = lax.dynamic_index_in_dim(groups, wide_index, 0, keepdims=False)
     own_slots = lax.dynamic_index_in_dim(slots, wide_index, 0, keepdims=False)
@@ -334,29 +358,38 @@
     def add(sets, density):
         return pair_terms(meta, energy, factors, sets, density)
 
-    def far_set(d, begin, with_direct):
+    def far_set(d, begin=0, end=3):
         parts = list(mirrored) if d == 0 else [pieces[d - 1] for pieces in forwarded]
-        parts = parts[begin:] + [far[d]] if with_direct else parts[begin:1]
-        return half + d, parts, begin * chunk
+        return half + d, (parts + [far[d]])[begin:end], begin * chunk
 
     density = add([(0, [factors], 0), (1, [near[0]], 0)], None)
     density = add([(d, [near[d - 1]], 0) for d in range(2, half)], density)
-    density = add([far_set(d, 0, True) for d in range(late)], density)
-    density = add([far_set(d, 0, False) for d in range(late, half)], density)
-
+    density = add([far_set(half - 1, 0, 1)], density)
+    density = add([far_set(d) for d in range(late)], density)
+    density = add([far_set(d) for d in range(late, half - 1)], density)
     keep, send = finish(
         meta, parity, energy, factors,
-        [far_set(d, 1, True) for d in range(late, half)], density, integrals, narrow_count,
+        [far_set(half - 1, 1)], density, integrals,
+        (wide_count, narrow_count),
     )
 
     x = keep + xor_permute(send, "narrow", 1).astype(F32)
-    for bit in bits_of(narrow_count)[1:]:
-        x = halve(x, "narrow", bit, highs["narrow", bit])
     tile = (auxiliary // wide_count, auxiliary // narrow_count)
-    x = x[0].T.reshape(wide_count, tile[0] * tile[1] // 128, 128)
-    for bit in bits_of(wide_count):
-        x = halve(x, "wide", bit, highs["wide", bit])
-    return x[0].reshape(tile)
+    packed = x.ndim == 4
+    if not packed:
+        x = x.transpose(0, 2, 1)
+    x = x.reshape(narrow_count // 2, 2, half, tile[0] * tile[1] // 128, 128)
+    y_bits = [("narrow", bit) for bit in bits_of(narrow_count)[1:]]
+    x_bits = [("wide", bit) for bit in bits_of(wide_count)[: len(y_bits)]]
+    paths = [x[:, 0], x[:, 1]]
+    for step in range(2 * len(y_bits)):
+        for p, order in enumerate([y_bits + x_bits, x_bits + y_bits]):
+            axis, bit = order[step]
+            paths[p] = halve(paths[p], axis, bit, highs[axis, bit], 0 if axis == "narrow" else 1)
+    x = jnp.concatenate(paths, axis=1)[0]
+    for bit in bits_of(wide_count)[len(y_bits) :]:
+        x = halve(x, "wide", bit, highs["wide", bit], 0)
+    return sparse_tile(x[0], highs["narrow", 1]) if packed else x[0].reshape(tile)
 
 
 def solution(mesh):

time: 183 us -> 178 us (0.973)
  starting transfers between devices: 47.2 us -> 32.8 us
  waiting for transfers between devices: 75.9 us -> 88.6 us
  Pallas kernels: 45.1 us -> 42 us
    ppermute x20 -> x22, starting transfers between devices: 47.2 us -> 32.8 us  [xor_permute(): lax.ppermute(x, axis, [(i, i ^ bit) for i in range(lax.axis_size(axis))])]
    ppermute x20 -> x22, waiting for transfers between devices: 75.9 us -> 88.6 us  [xor_permute(): lax.ppermute(x, axis, [(i, i ^ bit) for i in range(lax.axis_size(axis))])]
    pallas_call x1, Pallas kernels: 11.1 us -> 6.22 us  [finish(): pl.pallas_call(functools.partial(finish_kernel, static, steps, slab), out...]
    pallas_call x4 -> x5, Pallas kernels: 22.7 us -> 24.4 us  [pair_terms(): pl.pallas_call(functools.partial(pair_kernel, static, steps, initial), ou...]
    unnamed x29 -> x27, local copies, waits for them, and re-layouts: 5.3 us -> 5.33 us
  transfers between devices with their start and end apart: 20 -> 22, of which waited for: 9 -> 10; matrix products, arithmetic and copies ran while one was open for 3% -> 3% of each run, Pallas kernels for 17% -> 18%
where the time goes in v1:
time: 178 us; the launch traced here: 177 us
  waiting for transfers between devices  88.6 us (50%)
  Pallas kernels  42 us (24%)
  starting transfers between devices  32.8 us (18%)
  local copies, waits for them, and re-layouts  9.48 us (5%)
  other arithmetic  3.87 us (2%)
    ppermute x22, waiting for transfers between devices, xor_permute(): lax.ppermute(x, axis, [(i, i ^ bit) for i in range(lax.axis_size(axis))])  88.6 us
    ppermute x22, starting transfers between devices, xor_permute(): lax.ppermute(x, axis, [(i, i ^ bit) for i in range(lax.axis_size(axis))])  32.8 us
    pallas_call x5, Pallas kernels, pair_terms(): pl.pallas_call(functools.partial(pair_kernel, static, steps, initial), ou...  24.4 us
    pallas_call x4, Pallas kernels, take_pairs(): pl.pallas_call(functools.partial(take_kernel, base, (first, count)), out_...  11.4 us
    pallas_call x1, Pallas kernels, finish(): pl.pallas_call(functools.partial(finish_kernel, static, steps, slab), out...  6.22 us
    unnamed x27, local copies, waits for them, and re-layouts  5.33 us
  transfers between devices with their start and end apart: 22, of which 10 were waited for; matrix products, arithmetic and copies ran while one was open for 3% of the time, Pallas kernels for 18%

profile of v1, /device:TPU:0, one launch (start us, length us, event | category | flops | bytes accessed | tf_op | source)
XLA Modules:
  0.0 177.2 jit_solution(3866474006207890307)
XLA Ops:
  4.0 3.2 %take_pairs.7 = (bf16[2,256,768]{2,1,0:T(8,128)(2,1)}, bf16[2,256,768]{2,1,0:T(8,128)(2,1)}, bf16[2,256,768]{2,1,0:T(8,128)(2,1)}) custom-call(s32[32]{0:T(128)S(1)} %reshape.400.index_ref, bf16[6,256,768]{2,1,0:T(8,128)(2,1)S(1)} %copy-done), custom_call_target="tpu_custom_call" | custom-call | bytes 4718592 | tf_op jit(solution)/shard_map/take_pairs/pallas_call | solution.py:43
  7.2 3.0 %collective-permute-start.14 = (bf16[2,256,768]{2,1,0:T(8,128)(2,1)}, bf16[2,256,768]{2,1,0:T(8,128)(2,1)}, u32[]{:S(2)}, u32[]{:S(2)}) collective-permute-start(bf16[2,256,768]{2,1,0:T(8,128)(2,1)} %get-tuple-element.56), channel_id=1, source_target_pairs={{0,4},{4,0},{8,12},{12,8},{16,20},{20,16},{24,28},{28,24},{1,5},{5... | collective-permute-start | bytes 2359304 | tf_op jit(solution)/shard_map/ppermute | solution.py:19
  12.7 3.0 %collective-permute-start.2 = (bf16[6,64,768]{2,1,0:T(8,128)(2,1)}, bf16[6,64,768]{2,1,0:T(8,128)(2,1)}, u32[]{:S(2)}, u32[]{:S(2)}) collective-permute-start(bf16[6,64,768]{2,1,0:T(8,128)(2,1)} %slice.60), channel_id=1, source_target_pairs={{0,16},{4,20},{8,24},{12,28},{16,0},{20,4},{24,8},{28,12},{1,17},{... | collective-permute-start | bytes 1769480 | tf_op jit(solution)/shard_map/ppermute | solution.py:19
  18.2 41.4 %collective-permute-done.2.source_ref.refs_0_ = bf16[6,64,768]{2,1,0:T(8,128)(2,1)} collective-permute-done((bf16[6,64,768]{2,1,0:T(8,128)(2,1)}, bf16[6,64,768]{2,1,0:T(8,128)(2,1)}, u32[]{:S(2)}, u32[]{:S(2)}) %collective-permute-start.2) | collective-permute-done | bytes 589856 | tf_op jit(solution)/shard_map/ppermute | solution.py:19
  59.6 3.4 %take_pairs.5 = (bf16[2,112,768]{2,1,0:T(8,128)(2,1)}, bf16[2,112,768]{2,1,0:T(8,128)(2,1)}, bf16[2,112,768]{2,1,0:T(8,128)(2,1)S(1)}, bf16[2,112,768]{2,1,0:T(8,128)(2,1)S(1)}) custom-call(s32[32]{0:T(128)S(1)} %reshape.400.index_ref, bf16[6,256,768]{2,1,0:T(8,128)(2,1)S(1)} %copy-done.1), custom_call_target="tpu_custom_call" | custom-call | bytes 2752512 | tf_op jit(solution)/shard_map/take_pairs/pallas_call | solution.py:43
  64.4 3.4 %collective-permute-start.10 = (bf16[2,112,768]{2,1,0:T(8,128)(2,1)}, bf16[2,112,768]{2,1,0:T(8,128)(2,1)S(1)}, u32[]{:S(2)}, u32[]{:S(2)}) collective-permute-start(bf16[2,112,768]{2,1,0:T(8,128)(2,1)} %get-tuple-element.52), channel_id=1, source_target_pairs={{0,20},{4,16},{8,28},{12,24},{16,4},{20,0},{24,12},{28,8},{1,21},{... | collective-permute-start | bytes 1032200 | tf_op jit(solution)/shard_map/ppermute | solution.py:19
  67.8 7.6 %collective-permute-done.source_ref.refs_1_ = bf16[6,80,768]{2,1,0:T(8,128)(2,1)S(1)} collective-permute-done((bf16[6,80,768]{2,1,0:T(8,128)(2,1)}, bf16[6,80,768]{2,1,0:T(8,128)(2,1)S(1)}, u32[]{:S(2)}, u32[]{:S(2)}) %collective-permute-start) | collective-permute-done | bytes 737312 | tf_op jit(solution)/shard_map/ppermute | solution.py:19
  75.4 3.3 %collective-permute-start.7 = (bf16[2,112,768]{2,1,0:T(8,128)(2,1)}, bf16[2,112,768]{2,1,0:T(8,128)(2,1)}, u32[]{:S(2)}, u32[]{:S(2)}) collective-permute-start(bf16[2,112,768]{2,1,0:T(8,128)(2,1)} %get-tuple-element.49), channel_id=1, source_target_pairs={{0,16},{4,20},{8,24},{12,28},{16,0},{20,4},{24,8},{28,12},{1,17},{... | collective-permute-start | bytes 1032200 | tf_op jit(solution)/shard_map/ppermute | solution.py:19
  78.7 2.5 %take_pairs.6 = (bf16[2,64,768]{2,1,0:T(8,128)(2,1)}, bf16[2,64,768]{2,1,0:T(8,128)(2,1)S(1)}, bf16[2,64,768]{2,1,0:T(8,128)(2,1)}) custom-call(s32[32]{0:T(128)S(1)} %reshape.400.index_ref, bf16[6,64,768]{2,1,0:T(8,128)(2,1)} %collective-permute-done.2.source_ref.refs_0_), custom_call_target="tpu_custom_call" | custom-call | bytes 1179648 | tf_op jit(solution)/shard_map/take_pairs/pallas_call | solution.py:43
  81.3 2.3 %take_pairs.4 = (bf16[2,80,768]{2,1,0:T(8,128)(2,1)}, bf16[2,80,768]{2,1,0:T(8,128)(2,1)S(1)}, bf16[2,80,768]{2,1,0:T(8,128)(2,1)S(1)}) custom-call(s32[32]{0:T(128)S(1)} %reshape.400.index_ref, bf16[6,80,768]{2,1,0:T(8,128)(2,1)S(1)} %collective-permute-done.source_ref.refs_1_), custom_call_target="tpu_custom_call" | custom-call | bytes 1474560 | tf_op jit(solution)/shard_map/take_pairs/pallas_call | solution.py:43
  89.1 25.2 %collective-permute-done.11.refs_0_ = bf16[2,64,768]{2,1,0:T(8,128)(2,1)} collective-permute-done((bf16[2,64,768]{2,1,0:T(8,128)(2,1)}, bf16[2,64,768]{2,1,0:T(8,128)(2,1)}, u32[]{:S(2)}, u32[]{:S(2)}) %collective-permute-start.11) | collective-permute-done | bytes 196640 | tf_op jit(solution)/shard_map/ppermute | solution.py:19
  114.3 3.0 %collective-permute-start.6 = (bf16[2,112,768]{2,1,0:T(8,128)(2,1)}, bf16[2,112,768]{2,1,0:T(8,128)(2,1)S(1)}, u32[]{:S(2)}, u32[]{:S(2)}) collective-permute-start(bf16[2,112,768]{2,1,0:T(8,128)(2,1)} %copy-done.4), channel_id=1, source_target_pairs={{0,24},{4,28},{8,16},{12,20},{16,8},{20,12},{24,0},{28,4},{1,25},{... | collective-permute-start | bytes 1032200 | tf_op jit(solution)/shard_map/ppermute | solution.py:19
  117.4 5.3 %pair_terms.5.refs_2_ = f32[6,256,768]{2,1,0:T(8,128)S(1)} custom-call(s32[88]{0:T(128)S(1)} %reshape.398.meta_ref, f32[8,8,256]{2,1,0:T(8,128)S(1)} %bitcast.145, bf16[6,256,768]{2,1,0:T(8,128)(2,1)S(1)} %copy-done.1, bf16[6,256,768]{2,1,0:T(8,128)(2,1)S(1)} %copy-done.1, bf16[2,256,768]{2,1,0:T(8,128)(2,1)} %collective-permute-done.14.refs_1_), custom_call_target="tpu_custom_call" | custom-call | flops 1207959552 | bytes 1572864 | tf_op jit(solution)/shard_map/pair_terms/pallas_call | solution.py:141
  122.8 2.0 %collective-permute-start.5 = (bf16[2,80,768]{2,1,0:T(8,128)(2,1)S(1)}, bf16[2,80,768]{2,1,0:T(8,128)(2,1)S(1)}, u32[]{:S(2)}, u32[]{:S(2)}) collective-permute-start(bf16[2,80,768]{2,1,0:T(8,128)(2,1)S(1)} %copy-done.8), channel_id=1, source_target_pairs={{0,8},{4,12},{8,0},{12,4},{16,24},{20,28},{24,16},{28,20},{1,9},{5... | collective-permute-start | bytes 737288 | tf_op jit(solution)/shard_map/ppermute | solution.py:19
  126.6 5.8 %pair_terms.6.refs_1_ = f32[6,256,768]{2,1,0:T(8,128)S(1)} custom-call(s32[88]{0:T(128)S(1)} %reshape.398.meta_ref, f32[8,8,256]{2,1,0:T(8,128)S(1)} %bitcast.146, bf16[6,256,768]{2,1,0:T(8,128)(2,1)S(1)} %copy-done.1, bf16[2,256,768]{2,1,0:T(8,128)(2,1)} %collective-permute-done.12.refs_0_, ...), custom_call_target="tpu_custom_call", output_to_operand_aliasing={{}: (5, {})} | custom-call | flops 1207959552 | bytes 1572864 | tf_op jit(solution)/shard_map/pair_terms/pallas_call | solution.py:141
  132.4 3.4 %pair_terms.7.refs_6_ = f32[6,256,768]{2,1,0:T(8,128)S(1)} custom-call(s32[88]{0:T(128)S(1)} %reshape.398.meta_ref, f32[8,8,256]{2,1,0:T(8,128)S(1)} %bitcast.147, bf16[6,256,768]{2,1,0:T(8,128)(2,1)S(1)} %copy-done.1, bf16[2,64,768]{2,1,0:T(8,128)(2,1)} %collective-permute-done.11.refs_0_, ...), custom_call_target="tpu_custom_call", output_to_operand_aliasing={{}: (4, {})} | custom-call | flops 603979776 | bytes 786432 | tf_op jit(solution)/shard_map/pair_terms/pallas_call | solution.py:141
  135.8 6.3 %pair_terms.8.refs_3_ = f32[6,256,768]{2,1,0:T(8,128)S(1)} custom-call(s32[88]{0:T(128)S(1)} %reshape.398.meta_ref, f32[8,8,256]{2,1,0:T(8,128)S(1)} %bitcast.148, bf16[6,256,768]{2,1,0:T(8,128)(2,1)S(1)} %copy-done.1, bf16[6,64,768]{2,1,0:T(8,128)(2,1)} %collective-permute-done.2.source_ref.refs_0_, ...), custom_call_target="tpu_custom_call", output_to_operand_aliasing={{}: (9, {})} | custom-call | flops 1207959552 | bytes 1572864 | tf_op jit(solution)/shard_map/pair_terms/pallas_call | solution.py:141
  142.1 3.7 %pair_terms.9.refs_2_ = f32[6,256,768]{2,1,0:T(8,128)S(1)} custom-call(s32[88]{0:T(128)S(1)} %reshape.398.meta_ref, f32[8,8,256]{2,1,0:T(8,128)S(1)} %bitcast.149, bf16[6,256,768]{2,1,0:T(8,128)(2,1)S(1)} %copy-done.1, bf16[2,64,768]{2,1,0:T(8,128)(2,1)S(1)} %collective-permute-done.4.refs_0_, ...), custom_call_target="tpu_custom_call", output_to_operand_aliasing={{}: (6, {})} | custom-call | flops 603979776 | bytes 786432 | tf_op jit(solution)/shard_map/pair_terms/pallas_call | solution.py:141
  145.8 6.2 %finish.1 = (f32[2,8,144,128]{3,2,1,0:T(8,128)S(1)}, bf16[2,8,144,128]{3,2,1,0:T(8,128)(2,1)S(1)}, f32[6,256,768]{2,1,0:T(8,128)S(1)}) custom-call(s32[88]{0:T(128)S(1)} %reshape.398.meta_ref, s32[1]{0:T(128)} %bitcast.13.parity_ref, f32[8,8,256]{2,1,0:T(8,128)S(1)} %bitcast.150, ...), custom_call_target="tpu_custom_call", output_to_operand_aliasing={{2}: (6, {})} | custom-call | flops 1811939328 | bytes 7077888 | tf_op jit(solution)/shard_map/finish/pallas_call | solution.py:236
  156.5 3.8 %collective-permute-done.16 = bf16[1,4,144,128]{3,2,1,0:T(8,128)(2,1)S(1)} collective-permute-done((bf16[1,4,144,128]{3,2,1,0:T(8,128)(2,1)S(1)}, bf16[1,4,144,128]{3,2,1,0:T(8,128)(2,1)S(1)}, u32[]{:S(2)}, u32[]{:S(2)}) %collective-permute-start.16) | collective-permute-done | bytes 147488 | tf_op jit(solution)/shard_map/ppermute | solution.py:19
  162.6 2.2 %collective-permute-done.17 = bf16[1,2,144,128]{3,2,1,0:T(8,128)(2,1)S(1)} collective-permute-done((bf16[1,2,144,128]{3,2,1,0:T(8,128)(2,1)S(1)}, bf16[1,2,144,128]{3,2,1,0:T(8,128)(2,1)S(1)}, u32[]{:S(2)}, u32[]{:S(2)}) %collective-permute-start.17) | collective-permute-done | bytes 73760 | tf_op jit(solution)/shard_map/ppermute | solution.py:19
  166.2 2.0 %collective-permute-start.20 = (bf16[2,144,128]{2,1,0:T(8,128)(2,1)S(1)}, bf16[2,144,128]{2,1,0:T(8,128)(2,1)S(1)}, u32[]{:S(2)}, u32[]{:S(2)}) collective-permute-start(bf16[2,144,128]{2,1,0:T(8,128)(2,1)S(1)} %fusion.10), channel_id=1, source_target_pairs={{0,8},{4,12},{8,0},{12,4},{16,24},{20,28},{24,16},{28,20},{1,9},{5... | collective-permute-start | bytes 221192 | tf_op jit(solution)/shard_map/ppermute | solution.py:19
  168.2 2.4 %collective-permute-done.20 = bf16[2,144,128]{2,1,0:T(8,128)(2,1)S(1)} collective-permute-done((bf16[2,144,128]{2,1,0:T(8,128)(2,1)S(1)}, bf16[2,144,128]{2,1,0:T(8,128)(2,1)S(1)}, u32[]{:S(2)}, u32[]{:S(2)}) %collective-permute-start.20) | collective-permute-done | bytes 73760 | tf_op jit(solution)/shard_map/ppermute | solution.py:19
  170.6 3.8 %collective-permute-start.21 = (bf16[1,144,128]{2,1,0:T(8,128)(2,1)S(1)}, bf16[1,144,128]{2,1,0:T(8,128)(2,1)S(1)}, u32[]{:S(2)}, u32[]{:S(2)}) collective-permute-start(bf16[1,144,128]{2,1,0:T(8,128)(2,1)S(1)} %fusion.11), channel_id=1, source_target_pairs={{0,16},{4,20},{8,24},{12,28},{16,0},{20,4},{24,8},{28,12},{1,17},{... | collective-permute-start | bytes 110600 | tf_op jit(solution)/shard_map/ppermute | solution.py:19
  (115 shorter events, 28.6 us)
Async XLA Ops:
  4.0 13.4 %copy-start.12 = (f32[192]{0:T(256)S(1)}, f32[192]{0:T(256)}, u32[]{:S(2)}) copy-start(f32[192]{0:T(256)} %param.8) | copy-start | bytes 2308
  4.0 55.5 %copy-start.1 = (bf16[6,256,768]{2,1,0:T(8,128)(2,1)S(1)}, bf16[6,256,768]{2,1,0:T(8,128)(2,1)}, u32[]{:S(2)}) copy-start(bf16[6,256,768]{2,1,0:T(8,128)(2,1)} %factors_ref.11) | copy-start | bytes 7077892
  7.2 77.8 %collective-permute-start.14 = (bf16[2,256,768]{2,1,0:T(8,128)(2,1)}, bf16[2,256,768]{2,1,0:T(8,128)(2,1)}, u32[]{:S(2)}, u32[]{:S(2)}) collective-permute-start(bf16[2,256,768]{2,1,0:T(8,128)(2,1)} %get-tuple-element.56), channel_id=1, source_target_pairs={{0,4},{4,0},{8,12},{12,8},{16,20},{20,16},{24,28},{28,24},{1,5},{5... | collective-permute-start | bytes 2359304 | tf_op jit(solution)/shard_map/ppermute | solution.py:19
  10.2 74.9 %collective-permute-start.12 = (bf16[2,256,768]{2,1,0:T(8,128)(2,1)}, bf16[2,256,768]{2,1,0:T(8,128)(2,1)}, u32[]{:S(2)}, u32[]{:S(2)}) collective-permute-start(bf16[2,256,768]{2,1,0:T(8,128)(2,1)} %get-tuple-element.54), channel_id=1, source_target_pairs={{0,8},{4,12},{8,0},{12,4},{16,24},{20,28},{24,16},{28,20},{1,9},{5... | collective-permute-start | bytes 2359304 | tf_op jit(solution)/shard_map/ppermute | solution.py:19
  11.8 74.8 %collective-permute-start.13 = (bf16[2,256,768]{2,1,0:T(8,128)(2,1)}, bf16[2,256,768]{2,1,0:T(8,128)(2,1)}, u32[]{:S(2)}, u32[]{:S(2)}) collective-permute-start(bf16[2,256,768]{2,1,0:T(8,128)(2,1)} %get-tuple-element.55), channel_id=1, source_target_pairs={{0,12},{4,8},{8,4},{12,0},{16,28},{20,24},{24,20},{28,16},{1,13},{... | collective-permute-start | bytes 2359304 | tf_op jit(solution)/shard_map/ppermute | solution.py:19
  12.7 46.9 %collective-permute-start.2 = (bf16[6,64,768]{2,1,0:T(8,128)(2,1)}, bf16[6,64,768]{2,1,0:T(8,128)(2,1)}, u32[]{:S(2)}, u32[]{:S(2)}) collective-permute-start(bf16[6,64,768]{2,1,0:T(8,128)(2,1)} %slice.60), channel_id=1, source_target_pairs={{0,16},{4,20},{8,24},{12,28},{16,0},{20,4},{24,8},{28,12},{1,17},{... | collective-permute-start | bytes 1769480 | tf_op jit(solution)/shard_map/ppermute | solution.py:19
  16.6 58.8 %collective-permute-start = (bf16[6,80,768]{2,1,0:T(8,128)(2,1)}, bf16[6,80,768]{2,1,0:T(8,128)(2,1)S(1)}, u32[]{:S(2)}, u32[]{:S(2)}) collective-permute-start(bf16[6,80,768]{2,1,0:T(8,128)(2,1)} %slice.61), channel_id=1, source_target_pairs={{0,16},{4,20},{8,24},{12,28},{16,0},{20,4},{24,8},{28,12},{1,17},{... | collective-permute-start | bytes 2211848 | tf_op jit(solution)/shard_map/ppermute | solution.py:19
  64.4 58.3 %collective-permute-start.10 = (bf16[2,112,768]{2,1,0:T(8,128)(2,1)}, bf16[2,112,768]{2,1,0:T(8,128)(2,1)S(1)}, u32[]{:S(2)}, u32[]{:S(2)}) collective-permute-start(bf16[2,112,768]{2,1,0:T(8,128)(2,1)} %get-tuple-element.52), channel_id=1, source_target_pairs={{0,20},{4,16},{8,28},{12,24},{16,4},{20,0},{24,12},{28,8},{1,21},{... | collective-permute-start | bytes 1032200 | tf_op jit(solution)/shard_map/ppermute | solution.py:19
  75.4 47.4 %collective-permute-start.7 = (bf16[2,112,768]{2,1,0:T(8,128)(2,1)}, bf16[2,112,768]{2,1,0:T(8,128)(2,1)}, u32[]{:S(2)}, u32[]{:S(2)}) collective-permute-start(bf16[2,112,768]{2,1,0:T(8,128)(2,1)} %get-tuple-element.49), channel_id=1, source_target_pairs={{0,16},{4,20},{8,24},{12,28},{16,0},{20,4},{24,8},{28,12},{1,17},{... | collective-permute-start | bytes 1032200 | tf_op jit(solution)/shard_map/ppermute | solution.py:19
  85.0 29.2 %collective-permute-start.11 = (bf16[2,64,768]{2,1,0:T(8,128)(2,1)}, bf16[2,64,768]{2,1,0:T(8,128)(2,1)}, u32[]{:S(2)}, u32[]{:S(2)}) collective-permute-start(bf16[2,64,768]{2,1,0:T(8,128)(2,1)} %get-tuple-element.53), channel_id=1, source_target_pairs={{0,12},{4,8},{8,4},{12,0},{16,28},{20,24},{24,20},{28,16},{1,13},{... | collective-permute-start | bytes 589832 | tf_op jit(solution)/shard_map/ppermute | solution.py:19
  85.1 32.2 %collective-permute-start.8 = (bf16[2,64,768]{2,1,0:T(8,128)(2,1)}, bf16[2,64,768]{2,1,0:T(8,128)(2,1)}, u32[]{:S(2)}, u32[]{:S(2)}) collective-permute-start(bf16[2,64,768]{2,1,0:T(8,128)(2,1)} %get-tuple-element.50), channel_id=1, source_target_pairs={{0,4},{4,0},{8,12},{12,8},{16,20},{20,16},{24,28},{28,24},{1,5},{5... | collective-permute-start | bytes 589832 | tf_op jit(solution)/shard_map/ppermute | solution.py:19
  86.6 38.2 %collective-permute-start.9 = (bf16[2,80,768]{2,1,0:T(8,128)(2,1)}, bf16[2,80,768]{2,1,0:T(8,128)(2,1)}, u32[]{:S(2)}, u32[]{:S(2)}) collective-permute-start(bf16[2,80,768]{2,1,0:T(8,128)(2,1)} %get-tuple-element.51), channel_id=1, source_target_pairs={{0,4},{4,0},{8,12},{12,8},{16,20},{20,16},{24,28},{28,24},{1,5},{5... | collective-permute-start | bytes 737288 | tf_op jit(solution)/shard_map/ppermute | solution.py:19
  114.3 27.8 %collective-permute-start.6 = (bf16[2,112,768]{2,1,0:T(8,128)(2,1)}, bf16[2,112,768]{2,1,0:T(8,128)(2,1)S(1)}, u32[]{:S(2)}, u32[]{:S(2)}) collective-permute-start(bf16[2,112,768]{2,1,0:T(8,128)(2,1)} %copy-done.4), channel_id=1, source_target_pairs={{0,24},{4,28},{8,16},{12,20},{16,8},{20,12},{24,0},{28,4},{1,25},{... | collective-permute-start | bytes 1032200 | tf_op jit(solution)/shard_map/ppermute | solution.py:19
  117.3 28.5 %collective-permute-start.3 = (bf16[2,112,768]{2,1,0:T(8,128)(2,1)}, bf16[2,112,768]{2,1,0:T(8,128)(2,1)S(1)}, u32[]{:S(2)}, u32[]{:S(2)}) collective-permute-start(bf16[2,112,768]{2,1,0:T(8,128)(2,1)} %copy-done.3), channel_id=1, source_target_pairs={{0,28},{4,24},{8,20},{12,16},{16,12},{20,8},{24,4},{28,0},{1,29},{... | collective-permute-start | bytes 1032200 | tf_op jit(solution)/shard_map/ppermute | solution.py:19
  122.7 19.3 %collective-permute-start.4 = (bf16[2,64,768]{2,1,0:T(8,128)(2,1)S(1)}, bf16[2,64,768]{2,1,0:T(8,128)(2,1)S(1)}, u32[]{:S(2)}, u32[]{:S(2)}) collective-permute-start(bf16[2,64,768]{2,1,0:T(8,128)(2,1)S(1)} %copy-done.10), channel_id=1, source_target_pairs={{0,8},{4,12},{8,0},{12,4},{16,24},{20,28},{24,16},{28,20},{1,9},{5... | collective-permute-start | bytes 589832 | tf_op jit(solution)/shard_map/ppermute | solution.py:19
  122.8 19.2 %collective-permute-start.5 = (bf16[2,80,768]{2,1,0:T(8,128)(2,1)S(1)}, bf16[2,80,768]{2,1,0:T(8,128)(2,1)S(1)}, u32[]{:S(2)}, u32[]{:S(2)}) collective-permute-start(bf16[2,80,768]{2,1,0:T(8,128)(2,1)S(1)} %copy-done.8), channel_id=1, source_target_pairs={{0,8},{4,12},{8,0},{12,4},{16,24},{20,28},{24,16},{28,20},{1,9},{5... | collective-permute-start | bytes 737288 | tf_op jit(solution)/shard_map/ppermute | solution.py:19
  124.9 20.9 %collective-permute-start.1 = (bf16[2,80,768]{2,1,0:T(8,128)(2,1)S(1)}, bf16[2,80,768]{2,1,0:T(8,128)(2,1)S(1)}, u32[]{:S(2)}, u32[]{:S(2)}) collective-permute-start(bf16[2,80,768]{2,1,0:T(8,128)(2,1)S(1)} %copy-done.6), channel_id=1, source_target_pairs={{0,12},{4,8},{8,4},{12,0},{16,28},{20,24},{24,20},{28,16},{1,13},{... | collective-permute-start | bytes 737288 | tf_op jit(solution)/shard_map/ppermute | solution.py:19
  152.0 2.1 %collective-permute-start.15 = (bf16[2,8,144,128]{3,2,1,0:T(8,128)(2,1)S(1)}, bf16[2,8,144,128]{3,2,1,0:T(8,128)(2,1)S(1)}, u32[]{:S(2)}, u32[]{:S(2)}) collective-permute-start(bf16[2,8,144,128]{3,2,1,0:T(8,128)(2,1)S(1)} %get-tuple-element.58), channel_id=1, source_target_pairs={{0,1},{1,0},{2,3},{3,2},{4,5},{5,4},{6,7},{7,6},{8,9},{9,8},{10,11... | collective-permute-start | bytes 1769480 | tf_op jit(solution)/shard_map/ppermute | solution.py:19
  154.3 6.0 %collective-permute-start.16 = (bf16[1,4,144,128]{3,2,1,0:T(8,128)(2,1)S(1)}, bf16[1,4,144,128]{3,2,1,0:T(8,128)(2,1)S(1)}, u32[]{:S(2)}, u32[]{:S(2)}) collective-permute-start(bf16[1,4,144,128]{3,2,1,0:T(8,128)(2,1)S(1)} %fusion.1), channel_id=1, source_target_pairs={{0,2},{1,3},{2,0},{3,1},{4,6},{5,7},{6,4},{7,5},{8,10},{9,11},{10,... | collective-permute-start | bytes 442376 | tf_op jit(solution)/shard_map/ppermute | solution.py:19
  155.9 5.7 %collective-permute-start.18 = (bf16[2,2,144,128]{3,2,1,0:T(8,128)(2,1)S(1)}, bf16[2,2,144,128]{3,2,1,0:T(8,128)(2,1)S(1)}, u32[]{:S(2)}, u32[]{:S(2)}) collective-permute-start(bf16[2,2,144,128]{3,2,1,0:T(8,128)(2,1)S(1)} %fusion.2), channel_id=1, source_target_pairs={{0,4},{4,0},{8,12},{12,8},{16,20},{20,16},{24,28},{28,24},{1,5},{5... | collective-permute-start | bytes 442376 | tf_op jit(solution)/shard_map/ppermute | solution.py:19
  160.3 4.4 %collective-permute-start.17 = (bf16[1,2,144,128]{3,2,1,0:T(8,128)(2,1)S(1)}, bf16[1,2,144,128]{3,2,1,0:T(8,128)(2,1)S(1)}, u32[]{:S(2)}, u32[]{:S(2)}) collective-permute-start(bf16[1,2,144,128]{3,2,1,0:T(8,128)(2,1)S(1)} %fusion.8), channel_id=1, source_target_pairs={{0,4},{4,0},{8,12},{12,8},{16,20},{20,16},{24,28},{28,24},{1,5},{5... | collective-permute-start | bytes 221192 | tf_op jit(solution)/shard_map/ppermute | solution.py:19
  161.7 4.4 %collective-permute-start.19 = (bf16[1,2,144,128]{3,2,1,0:T(8,128)(2,1)S(1)}, bf16[1,2,144,128]{3,2,1,0:T(8,128)(2,1)S(1)}, u32[]{:S(2)}, u32[]{:S(2)}) collective-permute-start(bf16[1,2,144,128]{3,2,1,0:T(8,128)(2,1)S(1)} %fusion.9), channel_id=1, source_target_pairs={{0,2},{1,3},{2,0},{3,1},{4,6},{5,7},{6,4},{7,5},{8,10},{9,11},{10,... | collective-permute-start | bytes 221192 | tf_op jit(solution)/shard_map/ppermute | solution.py:19
  166.2 4.4 %collective-permute-start.20 = (bf16[2,144,128]{2,1,0:T(8,128)(2,1)S(1)}, bf16[2,144,128]{2,1,0:T(8,128)(2,1)S(1)}, u32[]{:S(2)}, u32[]{:S(2)}) collective-permute-start(bf16[2,144,128]{2,1,0:T(8,128)(2,1)S(1)} %fusion.10), channel_id=1, source_target_pairs={{0,8},{4,12},{8,0},{12,4},{16,24},{20,28},{24,16},{28,20},{1,9},{5... | collective-permute-start | bytes 221192 | tf_op jit(solution)/shard_map/ppermute | solution.py:19
  170.6 5.7 %collective-permute-start.21 = (bf16[1,144,128]{2,1,0:T(8,128)(2,1)S(1)}, bf16[1,144,128]{2,1,0:T(8,128)(2,1)S(1)}, u32[]{:S(2)}, u32[]{:S(2)}) collective-permute-start(bf16[1,144,128]{2,1,0:T(8,128)(2,1)S(1)} %fusion.11), channel_id=1, source_target_pairs={{0,16},{4,20},{8,24},{12,28},{16,0},{20,4},{24,8},{28,12},{1,17},{... | collective-permute-start | bytes 110600 | tf_op jit(solution)/shard_map/ppermute | solution.py:19
  (11 other events, 42.5 us)

commit v2 on v1

--- a/solution.py
+++ b/solution.py
@@ -20,44 +20,32 @@
 
 
 def take_kernel(base, rows, index_ref, source_ref, *refs):
-    outputs, (buffer, loaded, stored) = refs[:-3], refs[-3:]
+    outputs, sem = refs[:-1], refs[-1]
     first, count = rows
-    loads, stores = [], []
+    copies = []
     for k in range(2 * len(outputs)):
         lmo = source_ref.at[index_ref[base + k], pl.ds(first, count), :]
-        loads.append(pltpu.make_async_copy(lmo, buffer.at[k], loaded.at[k]))
-        target = outputs[k // 2].at[k % 2]
-        stores.append(pltpu.make_async_copy(buffer.at[k], target, stored.at[k]))
-    for load in loads:
-        load.start()
-    for load, store in zip(loads, stores):
-        load.wait()
-        store.start()
-    for store in stores:
-        store.wait()
-
-
-def take_pairs(source, index, base, outputs, first, count):
+        copies.append(pltpu.make_async_copy(lmo, outputs[k // 2].at[k % 2], sem.at[k]))
+    start_all(copies)
+    for copy in copies:
+        copy.wait()
+
+
+def take_pairs(source, index, base, outputs, first, count, limit=VMEM_LIMIT):
     auxiliary = source.shape[2]
-    any_spec = pl.BlockSpec(memory_space=pl.ANY)
     return pl.pallas_call(
         functools.partial(take_kernel, base, (first, count)),
-        out_shape=[jax.ShapeDtypeStruct((2, count, auxiliary), source.dtype)] * outputs,
-        grid_spec=pltpu.PrefetchScalarGridSpec(
-            num_scalar_prefetch=1,
-            grid=(1,),
-            in_specs=[pl.BlockSpec(memory_space=pltpu.HBM)],
-            out_specs=[any_spec] * outputs,
-            scratch_shapes=[
-                pltpu.VMEM((2 * outputs, count, auxiliary), source.dtype),
-                pltpu.SemaphoreType.DMA((2 * outputs,)),
-                pltpu.SemaphoreType.DMA((2 * outputs,)),
-            ],
-        ),
+        out_shape=[pltpu.VMEM((2, count, auxiliary), source.dtype)] * outputs,
+        in_specs=[
+            pl.BlockSpec(memory_space=pltpu.SMEM),
+            pl.BlockSpec(memory_space=pl.ANY),
+        ],
+        out_specs=[pl.BlockSpec(memory_space=pltpu.VMEM)] * outputs,
+        scratch_shapes=[pltpu.SemaphoreType.DMA((2 * outputs,))],
         cost_estimate=pl.CostEstimate(
             flops=0, transcendentals=0, bytes_accessed=8 * outputs * count * auxiliary
         ),
-        compiler_params=pltpu.CompilerParams(vmem_limit_bytes=VMEM_LIMIT),
+        compiler_params=pltpu.CompilerParams(vmem_limit_bytes=limit),
         name="take_pairs",
     )(index, source)
 
@@ -157,6 +145,46 @@
     )(meta, energy, factors, *parts, *([] if initial else [density]))
 
 
+def is_last_lmo(base, steps, meta_ref, lmo):
+    return functools.reduce(
+        jnp.logical_or, [meta_ref[base + 3 + 3 * k] == lmo for k in range(steps)]
+    )
+
+
+def add_total(total, integral, density):
+    total[...] += lax.dot_general(
+        integral, density.astype(BF16), (((0,), (0,)), ((), ())), preferred_element_type=F32
+    )
+
+
+def partial_kernel(base, steps, meta_ref, integrals_ref, density_ref, total_ref):
+    total_ref[...] = jnp.zeros_like(total_ref)
+    for i in range(density_ref.shape[0]):
+
+        @pl.when(jnp.logical_not(is_last_lmo(base, steps, meta_ref, i)))
+        def _():
+            add_total(total_ref, integrals_ref[i], density_ref[i])
+
+
+def partial_total(meta, group, density, integrals):
+    lmo_dev, orbitals, auxiliary = density.shape
+    steps = lmo_dev // 2
+    vmem_spec = pl.BlockSpec(memory_space=pltpu.VMEM)
+    return pl.pallas_call(
+        functools.partial(partial_kernel, (2 + 3 * steps) * group, steps),
+        out_shape=pltpu.VMEM((auxiliary, auxiliary), F32),
+        in_specs=[pl.BlockSpec(memory_space=pltpu.SMEM), vmem_spec, vmem_spec],
+        out_specs=vmem_spec,
+        cost_estimate=pl.CostEstimate(
+            flops=lmo_dev * orbitals * auxiliary * auxiliary,
+            transcendentals=0,
+            bytes_accessed=integrals.size,
+        ),
+        compiler_params=pltpu.CompilerParams(vmem_limit_bytes=VMEM_LIMIT),
+        name="partial_total",
+    )(meta, integrals, density)
+
+
 def dense_tiles(total, first, wide_count):
     rows = total.shape[0] // wide_count
     whole_even, middle, whole_odd = [
@@ -185,21 +213,15 @@
 def finish_kernel(sets, steps, slab, meta_ref, parity_ref, energy_ref, factors_ref, *refs):
     count = sum(len(counts) for *_, counts in sets)
     part_refs, refs = refs[:count], refs[count:]
-    _, integrals_ref, keep_ref, send_ref, density_ref = refs[:5]
-    buffers, (total, sem) = refs[5:-2], refs[-2:]
+    _, integrals_ref, _, keep_ref, send_ref, density_ref, total = refs[:7]
+    buffers, sem = refs[7:-1], refs[-1]
     copies = load_sets(sets, meta_ref, part_refs, buffers, sem)
     for group in copies:
         start_all(group)
     add_sets(sets, copies, buffers, steps, meta_ref, energy_ref, factors_ref, density_ref)
-    for i in range(density_ref.shape[0]):
-        term = lax.dot_general(
-            integrals_ref[i], density_ref[i].astype(BF16), (((0,), (0,)), ((), ())),
-            preferred_element_type=F32,
-        )
-        if i == 0:
-            total[...] = term
-        else:
-            total[...] += term
+    for k in range(steps):
+        lmo = meta_ref[sets[0][0] + 3 + 3 * k]
+        add_total(total, integrals_ref[lmo], density_ref[lmo])
     value = total[...]
     total[...] = 0.5 * (value + value.T)
     parity = parity_ref[0]
@@ -221,7 +243,7 @@
             send_ref[q] = even.astype(BF16)
 
 
-def finish(meta, parity, energy, factors, sets, density, integrals, counts):
+def finish(meta, parity, energy, factors, sets, density, integrals, total, counts):
     lmo_dev, orbitals, auxiliary = density.shape
     steps = lmo_dev // 2
     static, parts = set_shapes(sets, steps)
@@ -239,13 +261,14 @@
             pltpu.VMEM(out, F32),
             pltpu.VMEM(out, BF16),
             pltpu.VMEM(density.shape, F32),
+            pltpu.VMEM(total.shape, F32),
         ],
         in_specs=[smem_spec, smem_spec, vmem_spec, vmem_spec]
         + [vmem_spec] * len(parts)
-        + [vmem_spec, vmem_spec],
-        out_specs=[vmem_spec] * 3,
-        scratch_shapes=buffers + [pltpu.VMEM((auxiliary, auxiliary), F32), sem],
-        input_output_aliases={4 + len(parts): 2},
+        + [vmem_spec] * 3,
+        out_specs=[vmem_spec] * 4,
+        scratch_shapes=buffers + [sem],
+        input_output_aliases={4 + len(parts): 2, 6 + len(parts): 3},
         cost_estimate=pl.CostEstimate(
             flops=2 * lmo_dev * orbitals * auxiliary * auxiliary,
             transcendentals=0,
@@ -253,7 +276,7 @@
         ),
         compiler_params=pltpu.CompilerParams(vmem_limit_bytes=VMEM_LIMIT),
         name="finish",
-    )(meta, parity, energy, factors, *parts, density, integrals)[:2]
+    )(meta, parity, energy, factors, *parts, density, integrals, total)[:2]
 
 
 def halve(x, axis, bit, high, dim):
@@ -302,9 +325,10 @@
 
     asked = jnp.stack([asked_of(wide_index), asked_of(wide_index ^ half)]).reshape(-1)
 
+    limit = (64 << 20) - (half - 1) * 4 * orbitals * auxiliary - (3 << 19)
     near = [
         xor_permute(x, "wide", d + 1)
-        for d, x in enumerate(take_pairs(factors, asked, 2, half - 1, 0, orbitals))
+        for d, x in enumerate(take_pairs(factors, asked, 2, half - 1, 0, orbitals, limit))
     ]
     far_asked, mirrored[0] = lax.optimization_barrier((asked, mirrored[0]))
     far_rows = list(take_pairs(factors, far_asked, 2 * half, half, direct, orbitals - direct))
@@ -358,18 +382,18 @@
     def add(sets, density):
         return pair_terms(meta, energy, factors, sets, density)
 
-    def far_set(d, begin=0, end=3):
+    def far_set(d):
         parts = list(mirrored) if d == 0 else [pieces[d - 1] for pieces in forwarded]
-        return half + d, (parts + [far[d]])[begin:end], begin * chunk
+        return half + d, parts + [far[d]], 0
 
     density = add([(0, [factors], 0), (1, [near[0]], 0)], None)
     density = add([(d, [near[d - 1]], 0) for d in range(2, half)], density)
-    density = add([far_set(half - 1, 0, 1)], density)
     density = add([far_set(d) for d in range(late)], density)
     density = add([far_set(d) for d in range(late, half - 1)], density)
+    total = partial_total(meta, wide_count - 1, density, integrals)
     keep, send = finish(
         meta, parity, energy, factors,
-        [far_set(half - 1, 1)], density, integrals,
+        [far_set(half - 1)], density, integrals, total,
         (wide_count, narrow_count),
     )
 

time: 178 us -> 180 us (1.011)
  local copies, waits for them, and re-layouts: 9.48 us -> 13.6 us
  waiting for transfers between devices: 88.6 us -> 85.6 us
  starting transfers between devices: 32.8 us -> 35.4 us
    pallas_call x5 -> x4, Pallas kernels: 24.4 us -> 21 us  [pair_terms(): pl.pallas_call(functools.partial(pair_kernel, static, steps, initial), ou...]
    ppermute x22, waiting for transfers between devices: 88.6 us -> 85.6 us  [xor_permute(): lax.ppermute(x, axis, [(i, i ^ bit) for i in range(lax.axis_size(axis))])]
    ppermute x22, starting transfers between devices: 32.8 us -> 35.4 us  [xor_permute(): lax.ppermute(x, axis, [(i, i ^ bit) for i in range(lax.axis_size(axis))])]
    pallas_call x0 -> x1, Pallas kernels: none -> 2.27 us  [partial_total(): pl.pallas_call(functools.partial(partial_kernel, (2 + 3 * steps) * group,...]
    unnamed x27 -> x39, local copies, waits for them, and re-layouts: 5.33 us -> 6.71 us
  transfers between devices with their start and end apart: 22 -> 22, of which waited for: 10 -> 12; matrix products, arithmetic and copies ran while one was open for 3% -> 4% of each run, Pallas kernels for 18% -> 20%
where the time goes in v2:
time: 180 us
  waiting for transfers between devices  85.6 us (48%)
  Pallas kernels  40.7 us (23%)
  starting transfers between devices  35.4 us (20%)
  local copies, waits for them, and re-layouts  13.6 us (8%)
  other arithmetic  3.84 us (2%)
    ppermute x22, waiting for transfers between devices, xor_permute(): lax.ppermute(x, axis, [(i, i ^ bit) for i in range(lax.axis_size(axis))])  85.6 us
    ppermute x22, starting transfers between devices, xor_permute(): lax.ppermute(x, axis, [(i, i ^ bit) for i in range(lax.axis_size(axis))])  35.4 us
    pallas_call x4, Pallas kernels, pair_terms(): pl.pallas_call(functools.partial(pair_kernel, static, steps, initial), ou...  21 us
    pallas_call x4, Pallas kernels, take_pairs(): pl.pallas_call(functools.partial(take_kernel, base, (first, count)), out_...  11.8 us
    unnamed x39, local copies, waits for them, and re-layouts  6.71 us
    pallas_call x1, Pallas kernels, finish(): pl.pallas_call(functools.partial(finish_kernel, static, steps, slab), out...  5.62 us
  transfers between devices with their start and end apart: 22, of which 12 were waited for; matrix products, arithmetic and copies ran while one was open for 4% of the time, Pallas kernels for 20%

profile of v2, /device:TPU:0, one launch (start us, length us, event | category | flops | bytes accessed | tf_op | source)
XLA Modules:
  0.0 179.6 jit_solution(17422351306821120737)
XLA Ops:
  2.0 4.1 %collective-permute-start = (bf16[6,64,768]{2,1,0:T(8,128)(2,1)}, bf16[6,64,768]{2,1,0:T(8,128)(2,1)}, u32[]{:S(2)}, u32[]{:S(2)}) collective-permute-start(bf16[6,64,768]{2,1,0:T(8,128)(2,1)} %slice.60), channel_id=1, source_target_pairs={{0,16},{4,20},{8,24},{12,28},{16,0},{20,4},{24,8},{28,12},{1,17},{... | collective-permute-start | bytes 1769480 | tf_op jit(solution)/shard_map/ppermute | solution.py:19
  10.3 3.9 %take_pairs.7 = (bf16[2,256,768]{2,1,0:T(8,128)(2,1)}, bf16[2,256,768]{2,1,0:T(8,128)(2,1)}, bf16[2,256,768]{2,1,0:T(8,128)(2,1)}) custom-call(s32[32]{0:T(128)} %reshape.400.index_ref, bf16[6,256,768]{2,1,0:T(8,128)(2,1)} %factors_ref.9), custom_call_target="tpu_custom_call" | custom-call | bytes 4718592 | tf_op jit(solution)/shard_map/take_pairs/pallas_call | solution.py:36
  19.2 29.8 %collective-permute-done.source_ref.refs_0_ = bf16[6,64,768]{2,1,0:T(8,128)(2,1)} collective-permute-done((bf16[6,64,768]{2,1,0:T(8,128)(2,1)}, bf16[6,64,768]{2,1,0:T(8,128)(2,1)}, u32[]{:S(2)}, u32[]{:S(2)}) %collective-permute-start) | collective-permute-done | bytes 589856 | tf_op jit(solution)/shard_map/ppermute | solution.py:19
  49.1 2.4 %take_pairs.4 = (bf16[2,64,768]{2,1,0:T(8,128)(2,1)S(1)}, bf16[2,64,768]{2,1,0:T(8,128)(2,1)}, bf16[2,64,768]{2,1,0:T(8,128)(2,1)S(1)}) custom-call(s32[32]{0:T(128)S(1)} %copy-done.7, bf16[6,64,768]{2,1,0:T(8,128)(2,1)} %collective-permute-done.source_ref.refs_0_), custom_call_target="tpu_custom_call" | custom-call | bytes 1179648 | tf_op jit(solution)/shard_map/take_pairs/pallas_call | solution.py:36
  52.2 11.7 %collective-permute-done.2.source_ref.refs_1_ = bf16[6,80,768]{2,1,0:T(8,128)(2,1)S(1)} collective-permute-done((bf16[6,80,768]{2,1,0:T(8,128)(2,1)}, bf16[6,80,768]{2,1,0:T(8,128)(2,1)S(1)}, u32[]{:S(2)}, u32[]{:S(2)}) %collective-permute-start.2) | collective-permute-done | bytes 737312 | tf_op jit(solution)/shard_map/ppermute | solution.py:19
  67.1 3.3 %take_pairs.6 = (bf16[2,112,768]{2,1,0:T(8,128)(2,1)}, bf16[2,112,768]{2,1,0:T(8,128)(2,1)}, bf16[2,112,768]{2,1,0:T(8,128)(2,1)S(1)}, bf16[2,112,768]{2,1,0:T(8,128)(2,1)S(1)}) custom-call(s32[32]{0:T(128)S(1)} %copy-done.7, bf16[6,256,768]{2,1,0:T(8,128)(2,1)S(1)} %copy-done), custom_call_target="tpu_custom_call" | custom-call | bytes 2752512 | tf_op jit(solution)/shard_map/take_pairs/pallas_call | solution.py:36
  71.9 9.9 %collective-permute-done.5.refs_0_ = bf16[2,64,768]{2,1,0:T(8,128)(2,1)S(1)} collective-permute-done((bf16[2,64,768]{2,1,0:T(8,128)(2,1)}, bf16[2,64,768]{2,1,0:T(8,128)(2,1)S(1)}, u32[]{:S(2)}, u32[]{:S(2)}) %collective-permute-start.5) | collective-permute-done | bytes 196640 | tf_op jit(solution)/shard_map/ppermute | solution.py:19
  82.5 2.9 %collective-permute-start.8 = (bf16[2,112,768]{2,1,0:T(8,128)(2,1)}, bf16[2,112,768]{2,1,0:T(8,128)(2,1)}, u32[]{:S(2)}, u32[]{:S(2)}) collective-permute-start(bf16[2,112,768]{2,1,0:T(8,128)(2,1)} %get-tuple-element.50), channel_id=1, source_target_pairs={{0,16},{4,20},{8,24},{12,28},{16,0},{20,4},{24,8},{28,12},{1,17},{... | collective-permute-start | bytes 1032200 | tf_op jit(solution)/shard_map/ppermute | solution.py:19
  87.3 2.3 %take_pairs.5 = (bf16[2,80,768]{2,1,0:T(8,128)(2,1)}, bf16[2,80,768]{2,1,0:T(8,128)(2,1)S(1)}, bf16[2,80,768]{2,1,0:T(8,128)(2,1)S(1)}) custom-call(s32[32]{0:T(128)S(1)} %copy-done.7, bf16[6,80,768]{2,1,0:T(8,128)(2,1)S(1)} %collective-permute-done.2.source_ref.refs_1_), custom_call_target="tpu_custom_call" | custom-call | bytes 1474560 | tf_op jit(solution)/shard_map/take_pairs/pallas_call | solution.py:36
  91.0 4.6 %collective-permute-start.7 = (bf16[2,112,768]{2,1,0:T(8,128)(2,1)}, bf16[2,112,768]{2,1,0:T(8,128)(2,1)S(1)}, u32[]{:S(2)}, u32[]{:S(2)}) collective-permute-start(bf16[2,112,768]{2,1,0:T(8,128)(2,1)} %copy-done.10), channel_id=1, source_target_pairs={{0,24},{4,28},{8,16},{12,20},{16,8},{20,12},{24,0},{28,4},{1,25},{... | collective-permute-start | bytes 1032200 | tf_op jit(solution)/shard_map/ppermute | solution.py:19
  98.0 5.3 %pair_terms.4.refs_2_ = f32[6,256,768]{2,1,0:T(8,128)S(1)} custom-call(s32[88]{0:T(128)S(1)} %reshape.398.meta_ref, f32[8,8,256]{2,1,0:T(8,128)S(1)} %bitcast.145, bf16[6,256,768]{2,1,0:T(8,128)(2,1)S(1)} %copy-done.1, bf16[6,256,768]{2,1,0:T(8,128)(2,1)S(1)} %copy-done.1, bf16[2,256,768]{2,1,0:T(8,128)(2,1)} %collective-permute-done.14.refs_1_), custom_call_target="tpu_custom_call" | custom-call | flops 1207959552 | bytes 1572864 | tf_op jit(solution)/shard_map/pair_terms/pallas_call | solution.py:129
  103.3 13.2 %collective-permute-done.8.refs_2_ = bf16[2,112,768]{2,1,0:T(8,128)(2,1)} collective-permute-done((bf16[2,112,768]{2,1,0:T(8,128)(2,1)}, bf16[2,112,768]{2,1,0:T(8,128)(2,1)}, u32[]{:S(2)}, u32[]{:S(2)}) %collective-permute-start.8) | collective-permute-done | bytes 344096 | tf_op jit(solution)/shard_map/ppermute | solution.py:19
  116.6 2.7 %collective-permute-start.4 = (bf16[2,112,768]{2,1,0:T(8,128)(2,1)S(1)}, bf16[2,112,768]{2,1,0:T(8,128)(2,1)S(1)}, u32[]{:S(2)}, u32[]{:S(2)}) collective-permute-start(bf16[2,112,768]{2,1,0:T(8,128)(2,1)S(1)} %copy-done.9), channel_id=1, source_target_pairs={{0,28},{4,24},{8,20},{12,16},{16,12},{20,8},{24,4},{28,0},{1,29},{... | collective-permute-start | bytes 1032200 | tf_op jit(solution)/shard_map/ppermute | solution.py:19
  119.3 5.8 %pair_terms.5.refs_6_ = f32[6,256,768]{2,1,0:T(8,128)S(1)} custom-call(s32[88]{0:T(128)S(1)} %reshape.398.meta_ref, f32[8,8,256]{2,1,0:T(8,128)S(1)} %bitcast.146, bf16[6,256,768]{2,1,0:T(8,128)(2,1)S(1)} %copy-done.1, bf16[2,256,768]{2,1,0:T(8,128)(2,1)} %collective-permute-done.12.refs_0_, ...), custom_call_target="tpu_custom_call", output_to_operand_aliasing={{}: (5, {})} | custom-call | flops 1207959552 | bytes 1572864 | tf_op jit(solution)/shard_map/pair_terms/pallas_call | solution.py:129
  125.0 7.1 %collective-permute-done.11.refs_5_ = bf16[2,112,768]{2,1,0:T(8,128)(2,1)} collective-permute-done((bf16[2,112,768]{2,1,0:T(8,128)(2,1)}, bf16[2,112,768]{2,1,0:T(8,128)(2,1)}, u32[]{:S(2)}, u32[]{:S(2)}) %collective-permute-start.11) | collective-permute-done | bytes 344096 | tf_op jit(solution)/shard_map/ppermute | solution.py:19
  132.2 3.0 %collective-permute-start.3 = (bf16[2,80,768]{2,1,0:T(8,128)(2,1)S(1)}, bf16[2,80,768]{2,1,0:T(8,128)(2,1)S(1)}, u32[]{:S(2)}, u32[]{:S(2)}) collective-permute-start(bf16[2,80,768]{2,1,0:T(8,128)(2,1)S(1)} %copy-done.12), channel_id=1, source_target_pairs={{0,12},{4,8},{8,4},{12,0},{16,28},{20,24},{24,20},{28,16},{1,13},{... | collective-permute-start | bytes 737288 | tf_op jit(solution)/shard_map/ppermute | solution.py:19
  135.2 6.1 %pair_terms.6.refs_3_ = f32[6,256,768]{2,1,0:T(8,128)S(1)} custom-call(s32[88]{0:T(128)S(1)} %reshape.398.meta_ref, f32[8,8,256]{2,1,0:T(8,128)S(1)} %bitcast.147, bf16[6,256,768]{2,1,0:T(8,128)(2,1)S(1)} %copy-done.1, bf16[6,64,768]{2,1,0:T(8,128)(2,1)} %collective-permute-done.source_ref.refs_0_, ...), custom_call_target="tpu_custom_call", output_to_operand_aliasing={{}: (9, {})} | custom-call | flops 1207959552 | bytes 1572864 | tf_op jit(solution)/shard_map/pair_terms/pallas_call | solution.py:129
  141.3 3.8 %pair_terms.7.density_ref.refs_3_ = f32[6,256,768]{2,1,0:T(8,128)S(1)} custom-call(s32[88]{0:T(128)S(1)} %reshape.398.meta_ref, f32[8,8,256]{2,1,0:T(8,128)S(1)} %bitcast.148, bf16[6,256,768]{2,1,0:T(8,128)(2,1)S(1)} %copy-done.1, bf16[2,64,768]{2,1,0:T(8,128)(2,1)S(1)} %copy-done.6, ...), custom_call_target="tpu_custom_call", output_to_operand_aliasing={{}: (6, {})} | custom-call | flops 603979776 | bytes 786432 | tf_op jit(solution)/shard_map/pair_terms/pallas_call | solution.py:129
  145.1 2.3 %partial_total.1.refs_5_ = f32[768,768]{1,0:T(8,128)S(1)} custom-call(s32[88]{0:T(128)S(1)} %reshape.398.meta_ref, bf16[6,256,768]{2,1,0:T(8,128)(2,1)S(1)} %copy-done.2, f32[6,256,768]{2,1,0:T(8,128)S(1)} %pair_terms.7.density_ref.refs_3_), custom_call_target="tpu_custom_call" | custom-call | flops 905969664 | bytes 1179648 | tf_op jit(solution)/shard_map/partial_total/pallas_call | solution.py:173
  147.4 5.6 %finish.1 = (f32[2,8,144,128]{3,2,1,0:T(8,128)S(1)}, bf16[2,8,144,128]{3,2,1,0:T(8,128)(2,1)S(1)}, f32[6,256,768]{2,1,0:T(8,128)S(1)}, f32[768,768]{1,0:T(8,128)S(1)}) custom-call(s32[88]{0:T(128)S(1)} %reshape.398.meta_ref, s32[1]{0:T(128)} %bitcast.13.parity_ref, f32[8,8,256]{2,1,0:T(8,128)S(1)} %bitcast.149, ...), custom_call_target="tpu_custom_call", output_to_operand_aliasing={{2}: (7, {}), {3}: (9, {})} | custom-call | flops 1811939328 | bytes 7077888 | tf_op jit(solution)/shard_map/finish/pallas_call | solution.py:258
  157.6 3.7 %collective-permute-done.16 = bf16[1,4,144,128]{3,2,1,0:T(8,128)(2,1)S(1)} collective-permute-done((bf16[1,4,144,128]{3,2,1,0:T(8,128)(2,1)S(1)}, bf16[1,4,144,128]{3,2,1,0:T(8,128)(2,1)S(1)}, u32[]{:S(2)}, u32[]{:S(2)}) %collective-permute-start.16) | collective-permute-done | bytes 147488 | tf_op jit(solution)/shard_map/ppermute | solution.py:19
  167.0 3.5 %collective-permute-start.20 = (bf16[2,144,128]{2,1,0:T(8,128)(2,1)S(1)}, bf16[2,144,128]{2,1,0:T(8,128)(2,1)S(1)}, u32[]{:S(2)}, u32[]{:S(2)}) collective-permute-start(bf16[2,144,128]{2,1,0:T(8,128)(2,1)S(1)} %fusion.10), channel_id=1, source_target_pairs={{0,8},{4,12},{8,0},{12,4},{16,24},{20,28},{24,16},{28,20},{1,9},{5... | collective-permute-start | bytes 221192 | tf_op jit(solution)/shard_map/ppermute | solution.py:19
  170.6 2.3 %collective-permute-done.20 = bf16[2,144,128]{2,1,0:T(8,128)(2,1)S(1)} collective-permute-done((bf16[2,144,128]{2,1,0:T(8,128)(2,1)S(1)}, bf16[2,144,128]{2,1,0:T(8,128)(2,1)S(1)}, u32[]{:S(2)}, u32[]{:S(2)}) %collective-permute-start.20) | collective-permute-done | bytes 73760 | tf_op jit(solution)/shard_map/ppermute | solution.py:19
  172.9 3.9 %collective-permute-start.21 = (bf16[1,144,128]{2,1,0:T(8,128)(2,1)S(1)}, bf16[1,144,128]{2,1,0:T(8,128)(2,1)S(1)}, u32[]{:S(2)}, u32[]{:S(2)}) collective-permute-start(bf16[1,144,128]{2,1,0:T(8,128)(2,1)S(1)} %fusion.11), channel_id=1, source_target_pairs={{0,16},{4,20},{8,24},{12,28},{16,0},{20,4},{24,8},{28,12},{1,17},{... | collective-permute-start | bytes 110600 | tf_op jit(solution)/shard_map/ppermute | solution.py:19
  (127 shorter events, 35.9 us)
Async XLA Ops:
  2.0 47.1 %collective-permute-start = (bf16[6,64,768]{2,1,0:T(8,128)(2,1)}, bf16[6,64,768]{2,1,0:T(8,128)(2,1)}, u32[]{:S(2)}, u32[]{:S(2)}) collective-permute-start(bf16[6,64,768]{2,1,0:T(8,128)(2,1)} %slice.60), channel_id=1, source_target_pairs={{0,16},{4,20},{8,24},{12,28},{16,0},{20,4},{24,8},{28,12},{1,17},{... | collective-permute-start | bytes 1769480 | tf_op jit(solution)/shard_map/ppermute | solution.py:19
  8.0 55.9 %collective-permute-start.2 = (bf16[6,80,768]{2,1,0:T(8,128)(2,1)}, bf16[6,80,768]{2,1,0:T(8,128)(2,1)S(1)}, u32[]{:S(2)}, u32[]{:S(2)}) collective-permute-start(bf16[6,80,768]{2,1,0:T(8,128)(2,1)} %slice.61), channel_id=1, source_target_pairs={{0,16},{4,20},{8,24},{12,28},{16,0},{20,4},{24,8},{28,12},{1,17},{... | collective-permute-start | bytes 2211848 | tf_op jit(solution)/shard_map/ppermute | solution.py:19
  10.3 38.7 %copy-start.7 = (s32[32]{0:T(128)S(1)}, s32[32]{0:T(128)}, u32[]{:S(2)}) copy-start(s32[32]{0:T(128)} %reshape.400.index_ref) | copy-start | bytes 388
  14.2 76.8 %collective-permute-start.12 = (bf16[2,256,768]{2,1,0:T(8,128)(2,1)}, bf16[2,256,768]{2,1,0:T(8,128)(2,1)}, u32[]{:S(2)}, u32[]{:S(2)}) collective-permute-start(bf16[2,256,768]{2,1,0:T(8,128)(2,1)} %get-tuple-element.54), channel_id=1, source_target_pairs={{0,8},{4,12},{8,0},{12,4},{16,24},{20,28},{24,16},{28,20},{1,9},{5... | collective-permute-start | bytes 2359304 | tf_op jit(solution)/shard_map/ppermute | solution.py:19
  16.1 79.5 %collective-permute-start.13 = (bf16[2,256,768]{2,1,0:T(8,128)(2,1)}, bf16[2,256,768]{2,1,0:T(8,128)(2,1)}, u32[]{:S(2)}, u32[]{:S(2)}) collective-permute-start(bf16[2,256,768]{2,1,0:T(8,128)(2,1)} %get-tuple-element.55), channel_id=1, source_target_pairs={{0,12},{4,8},{8,4},{12,0},{16,28},{20,24},{24,20},{28,16},{1,13},{... | collective-permute-start | bytes 2359304 | tf_op jit(solution)/shard_map/ppermute | solution.py:19
  17.5 80.4 %collective-permute-start.14 = (bf16[2,256,768]{2,1,0:T(8,128)(2,1)}, bf16[2,256,768]{2,1,0:T(8,128)(2,1)}, u32[]{:S(2)}, u32[]{:S(2)}) collective-permute-start(bf16[2,256,768]{2,1,0:T(8,128)(2,1)} %get-tuple-element.56), channel_id=1, source_target_pairs={{0,4},{4,0},{8,12},{12,8},{16,20},{20,16},{24,28},{28,24},{1,5},{5... | collective-permute-start | bytes 2359304 | tf_op jit(solution)/shard_map/ppermute | solution.py:19
  52.1 29.7 %collective-permute-start.5 = (bf16[2,64,768]{2,1,0:T(8,128)(2,1)}, bf16[2,64,768]{2,1,0:T(8,128)(2,1)S(1)}, u32[]{:S(2)}, u32[]{:S(2)}) collective-permute-start(bf16[2,64,768]{2,1,0:T(8,128)(2,1)} %get-tuple-element.47), channel_id=1, source_target_pairs={{0,8},{4,12},{8,0},{12,4},{16,24},{20,28},{24,16},{28,20},{1,9},{5... | collective-permute-start | bytes 589832 | tf_op jit(solution)/shard_map/ppermute | solution.py:19
  63.9 21.5 %collective-permute-start.9 = (bf16[2,64,768]{2,1,0:T(8,128)(2,1)S(1)}, bf16[2,64,768]{2,1,0:T(8,128)(2,1)S(1)}, u32[]{:S(2)}, u32[]{:S(2)}) collective-permute-start(bf16[2,64,768]{2,1,0:T(8,128)(2,1)S(1)} %get-tuple-element.51), channel_id=1, source_target_pairs={{0,4},{4,0},{8,12},{12,8},{16,20},{20,16},{24,28},{28,24},{1,5},{5... | collective-permute-start | bytes 589832 | tf_op jit(solution)/shard_map/ppermute | solution.py:19
  67.1 30.9 %copy-start.1 = (bf16[6,256,768]{2,1,0:T(8,128)(2,1)S(1)}, bf16[6,256,768]{2,1,0:T(8,128)(2,1)}, u32[]{:S(2)}) copy-start(bf16[6,256,768]{2,1,0:T(8,128)(2,1)} %factors_ref.9) | copy-start | bytes 7077892
  82.5 34.1 %collective-permute-start.8 = (bf16[2,112,768]{2,1,0:T(8,128)(2,1)}, bf16[2,112,768]{2,1,0:T(8,128)(2,1)}, u32[]{:S(2)}, u32[]{:S(2)}) collective-permute-start(bf16[2,112,768]{2,1,0:T(8,128)(2,1)} %get-tuple-element.50), channel_id=1, source_target_pairs={{0,16},{4,20},{8,24},{12,28},{16,0},{20,4},{24,8},{28,12},{1,17},{... | collective-permute-start | bytes 1032200 | tf_op jit(solution)/shard_map/ppermute | solution.py:19
  86.1 46.1 %collective-permute-start.11 = (bf16[2,112,768]{2,1,0:T(8,128)(2,1)}, bf16[2,112,768]{2,1,0:T(8,128)(2,1)}, u32[]{:S(2)}, u32[]{:S(2)}) collective-permute-start(bf16[2,112,768]{2,1,0:T(8,128)(2,1)} %get-tuple-element.53), channel_id=1, source_target_pairs={{0,20},{4,16},{8,28},{12,24},{16,4},{20,0},{24,12},{28,8},{1,21},{... | collective-permute-start | bytes 1032200 | tf_op jit(solution)/shard_map/ppermute | solution.py:19
  91.0 50.2 %collective-permute-start.7 = (bf16[2,112,768]{2,1,0:T(8,128)(2,1)}, bf16[2,112,768]{2,1,0:T(8,128)(2,1)S(1)}, u32[]{:S(2)}, u32[]{:S(2)}) collective-permute-start(bf16[2,112,768]{2,1,0:T(8,128)(2,1)} %copy-done.10), channel_id=1, source_target_pairs={{0,24},{4,28},{8,16},{12,20},{16,8},{20,12},{24,0},{28,4},{1,25},{... | collective-permute-start | bytes 1032200 | tf_op jit(solution)/shard_map/ppermute | solution.py:19
  95.6 36.5 %collective-permute-start.10 = (bf16[2,80,768]{2,1,0:T(8,128)(2,1)}, bf16[2,80,768]{2,1,0:T(8,128)(2,1)}, u32[]{:S(2)}, u32[]{:S(2)}) collective-permute-start(bf16[2,80,768]{2,1,0:T(8,128)(2,1)} %get-tuple-element.52), channel_id=1, source_target_pairs={{0,4},{4,0},{8,12},{12,8},{16,20},{20,16},{24,28},{28,24},{1,5},{5... | collective-permute-start | bytes 737288 | tf_op jit(solution)/shard_map/ppermute | solution.py:19
  97.9 43.4 %collective-permute-start.6 = (bf16[2,80,768]{2,1,0:T(8,128)(2,1)}, bf16[2,80,768]{2,1,0:T(8,128)(2,1)S(1)}, u32[]{:S(2)}, u32[]{:S(2)}) collective-permute-start(bf16[2,80,768]{2,1,0:T(8,128)(2,1)} %copy-done.13), channel_id=1, source_target_pairs={{0,8},{4,12},{8,0},{12,4},{16,24},{20,28},{24,16},{28,20},{1,9},{5... | collective-permute-start | bytes 737288 | tf_op jit(solution)/shard_map/ppermute | solution.py:19
  116.6 30.8 %collective-permute-start.4 = (bf16[2,112,768]{2,1,0:T(8,128)(2,1)S(1)}, bf16[2,112,768]{2,1,0:T(8,128)(2,1)S(1)}, u32[]{:S(2)}, u32[]{:S(2)}) collective-permute-start(bf16[2,112,768]{2,1,0:T(8,128)(2,1)S(1)} %copy-done.9), channel_id=1, source_target_pairs={{0,28},{4,24},{8,20},{12,16},{16,12},{20,8},{24,4},{28,0},{1,29},{... | collective-permute-start | bytes 1032200 | tf_op jit(solution)/shard_map/ppermute | solution.py:19
  132.2 15.3 %collective-permute-start.1 = (bf16[2,64,768]{2,1,0:T(8,128)(2,1)S(1)}, bf16[2,64,768]{2,1,0:T(8,128)(2,1)S(1)}, u32[]{:S(2)}, u32[]{:S(2)}) collective-permute-start(bf16[2,64,768]{2,1,0:T(8,128)(2,1)S(1)} %copy-done.15), channel_id=1, source_target_pairs={{0,12},{4,8},{8,4},{12,0},{16,28},{20,24},{24,20},{28,16},{1,13},{... | collective-permute-start | bytes 589832 | tf_op jit(solution)/shard_map/ppermute | solution.py:19
  132.2 15.2 %collective-permute-start.3 = (bf16[2,80,768]{2,1,0:T(8,128)(2,1)S(1)}, bf16[2,80,768]{2,1,0:T(8,128)(2,1)S(1)}, u32[]{:S(2)}, u32[]{:S(2)}) collective-permute-start(bf16[2,80,768]{2,1,0:T(8,128)(2,1)S(1)} %copy-done.12), channel_id=1, source_target_pairs={{0,12},{4,8},{8,4},{12,0},{16,28},{20,24},{24,20},{28,16},{1,13},{... | collective-permute-start | bytes 737288 | tf_op jit(solution)/shard_map/ppermute | solution.py:19
  153.1 2.1 %collective-permute-start.15 = (bf16[2,8,144,128]{3,2,1,0:T(8,128)(2,1)S(1)}, bf16[2,8,144,128]{3,2,1,0:T(8,128)(2,1)S(1)}, u32[]{:S(2)}, u32[]{:S(2)}) collective-permute-start(bf16[2,8,144,128]{3,2,1,0:T(8,128)(2,1)S(1)} %get-tuple-element.58), channel_id=1, source_target_pairs={{0,1},{1,0},{2,3},{3,2},{4,5},{5,4},{6,7},{7,6},{8,9},{9,8},{10,11... | collective-permute-start | bytes 1769480 | tf_op jit(solution)/shard_map/ppermute | solution.py:19
  155.4 6.0 %collective-permute-start.16 = (bf16[1,4,144,128]{3,2,1,0:T(8,128)(2,1)S(1)}, bf16[1,4,144,128]{3,2,1,0:T(8,128)(2,1)S(1)}, u32[]{:S(2)}, u32[]{:S(2)}) collective-permute-start(bf16[1,4,144,128]{3,2,1,0:T(8,128)(2,1)S(1)} %fusion.1), channel_id=1, source_target_pairs={{0,2},{1,3},{2,0},{3,1},{4,6},{5,7},{6,4},{7,5},{8,10},{9,11},{10,... | collective-permute-start | bytes 442376 | tf_op jit(solution)/shard_map/ppermute | solution.py:19
  156.8 5.7 %collective-permute-start.18 = (bf16[2,2,144,128]{3,2,1,0:T(8,128)(2,1)S(1)}, bf16[2,2,144,128]{3,2,1,0:T(8,128)(2,1)S(1)}, u32[]{:S(2)}, u32[]{:S(2)}) collective-permute-start(bf16[2,2,144,128]{3,2,1,0:T(8,128)(2,1)S(1)} %fusion.2), channel_id=1, source_target_pairs={{0,4},{4,0},{8,12},{12,8},{16,20},{20,16},{24,28},{28,24},{1,5},{5... | collective-permute-start | bytes 442376 | tf_op jit(solution)/shard_map/ppermute | solution.py:19
  161.4 4.4 %collective-permute-start.17 = (bf16[1,2,144,128]{3,2,1,0:T(8,128)(2,1)S(1)}, bf16[1,2,144,128]{3,2,1,0:T(8,128)(2,1)S(1)}, u32[]{:S(2)}, u32[]{:S(2)}) collective-permute-start(bf16[1,2,144,128]{3,2,1,0:T(8,128)(2,1)S(1)} %fusion.8), channel_id=1, source_target_pairs={{0,4},{4,0},{8,12},{12,8},{16,20},{20,16},{24,28},{28,24},{1,5},{5... | collective-permute-start | bytes 221192 | tf_op jit(solution)/shard_map/ppermute | solution.py:19
  162.5 4.4 %collective-permute-start.19 = (bf16[1,2,144,128]{3,2,1,0:T(8,128)(2,1)S(1)}, bf16[1,2,144,128]{3,2,1,0:T(8,128)(2,1)S(1)}, u32[]{:S(2)}, u32[]{:S(2)}) collective-permute-start(bf16[1,2,144,128]{3,2,1,0:T(8,128)(2,1)S(1)} %fusion.9), channel_id=1, source_target_pairs={{0,2},{1,3},{2,0},{3,1},{4,6},{5,7},{6,4},{7,5},{8,10},{9,11},{10,... | collective-permute-start | bytes 221192 | tf_op jit(solution)/shard_map/ppermute | solution.py:19
  167.0 5.8 %collective-permute-start.20 = (bf16[2,144,128]{2,1,0:T(8,128)(2,1)S(1)}, bf16[2,144,128]{2,1,0:T(8,128)(2,1)S(1)}, u32[]{:S(2)}, u32[]{:S(2)}) collective-permute-start(bf16[2,144,128]{2,1,0:T(8,128)(2,1)S(1)} %fusion.10), channel_id=1, source_target_pairs={{0,8},{4,12},{8,0},{12,4},{16,24},{20,28},{24,16},{28,20},{1,9},{5... | collective-permute-start | bytes 221192 | tf_op jit(solution)/shard_map/ppermute | solution.py:19
  172.9 5.8 %collective-permute-start.21 = (bf16[1,144,128]{2,1,0:T(8,128)(2,1)S(1)}, bf16[1,144,128]{2,1,0:T(8,128)(2,1)S(1)}, u32[]{:S(2)}, u32[]{:S(2)}) collective-permute-start(bf16[1,144,128]{2,1,0:T(8,128)(2,1)S(1)} %fusion.11), channel_id=1, source_target_pairs={{0,16},{4,20},{8,24},{12,28},{16,0},{20,4},{24,8},{28,12},{1,17},{... | collective-permute-start | bytes 110600 | tf_op jit(solution)/shard_map/ppermute | solution.py:19
  (17 other events, 128.5 us)

commit v3 on v2

--- a/solution.py
+++ b/solution.py
@@ -12,7 +12,7 @@
 F32 = jnp.float32
 BF16 = jnp.bfloat16
 VMEM_LIMIT = 24 << 20
-MIRRORED_ROWS = (64, 144)
+MIRRORED_ROWS = (64, 160)
 
 
 def xor_permute(x, axis, bit):
@@ -29,6 +29,57 @@
     start_all(copies)
     for copy in copies:
         copy.wait()
+
+
+def take_near_kernel(offsets, lmo_dev, partners_ref, source_ref, *refs):
+    outputs, (buffer, loaded, stored) = refs[:-3], refs[-3:]
+    narrow_count = lax.axis_size("narrow")
+    wide_index, narrow_index = lax.axis_index("wide"), lax.axis_index("narrow")
+    first = (wide_index * narrow_count + narrow_index) * lmo_dev
+    loads, stores = [], []
+    for number, offset in enumerate(offsets):
+        asker = ((wide_index ^ offset) * narrow_count + narrow_index) * lmo_dev
+        low, high = jnp.int32(lmo_dev - 1), jnp.int32(0)
+        for i in range(lmo_dev):
+            for k in range(PARTNERS):
+                slot = partners_ref[k, asker + i] - first
+                hit = jnp.logical_and(slot >= 0, slot < lmo_dev)
+                low = jnp.where(hit, jnp.minimum(low, slot), low)
+                high = jnp.where(hit, jnp.maximum(high, slot), high)
+        for r, slot in enumerate((low, high)):
+            k = 2 * number + r
+            loads.append(pltpu.make_async_copy(source_ref.at[slot], buffer.at[k], loaded.at[k]))
+            stores.append(
+                pltpu.make_async_copy(buffer.at[k], outputs[number].at[r], stored.at[k])
+            )
+            loads[-1].start()
+    for load, store in zip(loads, stores):
+        load.wait()
+        store.start()
+    for store in stores:
+        store.wait()
+
+
+def take_near(source, partners, offsets, limit):
+    lmo_dev, orbitals, auxiliary = source.shape
+    count = len(offsets)
+    any_spec = pl.BlockSpec(memory_space=pl.ANY)
+    return pl.pallas_call(
+        functools.partial(take_near_kernel, offsets, lmo_dev),
+        out_shape=[jax.ShapeDtypeStruct((2, orbitals, auxiliary), source.dtype)] * count,
+        in_specs=[pl.BlockSpec(memory_space=pltpu.SMEM), any_spec],
+        out_specs=[any_spec] * count,
+        scratch_shapes=[
+            pltpu.VMEM((2 * count, orbitals, auxiliary), source.dtype),
+            pltpu.SemaphoreType.DMA((2 * count,)),
+            pltpu.SemaphoreType.DMA((2 * count,)),
+        ],
+        cost_estimate=pl.CostEstimate(
+            flops=0, transcendentals=0, bytes_accessed=8 * count * orbitals * auxiliary
+        ),
+        compiler_params=pltpu.CompilerParams(vmem_limit_bytes=limit),
+        name="take_near",
+    )(partners.T, source)
 
 
 def take_pairs(source, index, base, outputs, first, count, limit=VMEM_LIMIT):
@@ -325,11 +376,11 @@
 
     asked = jnp.stack([asked_of(wide_index), asked_of(wide_index ^ half)]).reshape(-1)
 
-    limit = (64 << 20) - (half - 1) * 4 * orbitals * auxiliary - (3 << 19)
-    near = [
-        xor_permute(x, "wide", d + 1)
-        for d, x in enumerate(take_pairs(factors, asked, 2, half - 1, 0, orbitals, limit))
-    ]
+    limit = (64 << 20) - (3 << 19)
+    offsets = tuple(range(2, half)) + (1,)
+    near = [None] * (half - 1)
+    for d, x in zip(offsets, take_near(factors, partners, offsets, limit)):
+        near[d - 1] = xor_permute(x, "wide", d)
     far_asked, mirrored[0] = lax.optimization_barrier((asked, mirrored[0]))
     far_rows = list(take_pairs(factors, far_asked, 2 * half, half, direct, orbitals - direct))
     late = half // 2
@@ -386,8 +437,8 @@
         parts = list(mirrored) if d == 0 else [pieces[d - 1] for pieces in forwarded]
         return half + d, parts + [far[d]], 0
 
-    density = add([(0, [factors], 0), (1, [near[0]], 0)], None)
-    density = add([(d, [near[d - 1]], 0) for d in range(2, half)], density)
+    density = add([(0, [factors], 0)], None)
+    density = add([(d, [near[d - 1]], 0) for d in range(1, half)], density)
     density = add([far_set(d) for d in range(late)], density)
     density = add([far_set(d) for d in range(late, half - 1)], density)
     total = partial_total(meta, wide_count - 1, density, integrals)
@@ -411,8 +462,15 @@
             axis, bit = order[step]
             paths[p] = halve(paths[p], axis, bit, highs[axis, bit], 0 if axis == "narrow" else 1)
     x = jnp.concatenate(paths, axis=1)[0]
-    for bit in bits_of(wide_count)[len(y_bits) :]:
-        x = halve(x, "wide", bit, highs["wide", bit], 0)
+    rest = bits_of(wide_count)[len(y_bits) :]
+    for bit in rest:
+        step = bit // rest[0]
+        pairs = x.reshape((x.shape[0] // (2 * step), 2, step) + x.shape[1:])
+        x = jnp.where(highs["wide", bit], pairs[:, ::-1], pairs).reshape(x.shape)
+    total = x[0]
+    for offset in range(x.shape[0] - 1, 0, -1):
+        total += xor_permute(x[offset].astype(BF16), "wide", offset * rest[0]).astype(F32)
+    x = total[None]
     return sparse_tile(x[0], highs["narrow", 1]) if packed else x[0].reshape(tile)
 
 

time: 180 us -> 184 us (1.022)
  waiting for transfers between devices: 85.6 us -> 94.4 us
  starting transfers between devices: 35.4 us -> 31.7 us
  local copies, waits for them, and re-layouts: 13.6 us -> 11.1 us
    ppermute x22 -> x23, waiting for transfers between devices: 85.6 us -> 94.4 us  [xor_permute(): lax.ppermute(x, axis, [(i, i ^ bit) for i in range(lax.axis_size(axis))])]
    pallas_call x4 -> x3, Pallas kernels: 11.8 us -> 7.85 us  [take_pairs(): pl.pallas_call(functools.partial(take_kernel, base, (first, count)), out_...]
    pallas_call x0 -> x1, Pallas kernels: none -> 3.87 us  [take_near(): pl.pallas_call(functools.partial(take_near_kernel, offsets, lmo_dev), out...]
    ppermute x22 -> x23, starting transfers between devices: 35.4 us -> 31.7 us  [xor_permute(): lax.ppermute(x, axis, [(i, i ^ bit) for i in range(lax.axis_size(axis))])]
    unnamed x39 -> x31, local copies, waits for them, and re-layouts: 6.71 us -> 4.62 us
  transfers between devices with their start and end apart: 22 -> 23, of which waited for: 12 -> 13; matrix products, arithmetic and copies ran while one was open for 4% -> 5% of each run, Pallas kernels for 20% -> 19%
where the time goes in v3:
time: 184 us; the launch traced here: 183 us
  waiting for transfers between devices  94.4 us (51%)
  Pallas kernels  40.7 us (22%)
  starting transfers between devices  31.7 us (17%)
  local copies, waits for them, and re-layouts  11.1 us (6%)
  other arithmetic  4.83 us (3%)
    ppermute x23, waiting for transfers between devices, xor_permute(): lax.ppermute(x, axis, [(i, i ^ bit) for i in range(lax.axis_size(axis))])  94.4 us
    ppermute x23, starting transfers between devices, xor_permute(): lax.ppermute(x, axis, [(i, i ^ bit) for i in range(lax.axis_size(axis))])  31.7 us
    pallas_call x4, Pallas kernels, pair_terms(): pl.pallas_call(functools.partial(pair_kernel, static, steps, initial), ou...  21.1 us
    pallas_call x3, Pallas kernels, take_pairs(): pl.pallas_call(functools.partial(take_kernel, base, (first, count)), out_...  7.85 us
    pallas_call x1, Pallas kernels, finish(): pl.pallas_call(functools.partial(finish_kernel, static, steps, slab), out...  5.62 us
    unnamed x31, local copies, waits for them, and re-layouts  4.62 us
    pallas_call x1, Pallas kernels, take_near(): pl.pallas_call(functools.partial(take_near_kernel, offsets, lmo_dev), out...  3.87 us
  transfers between devices with their start and end apart: 23, of which 13 were waited for; matrix products, arithmetic and copies ran while one was open for 5% of the time, Pallas kernels for 19%

profile of v3, /device:TPU:0, one launch (start us, length us, event | category | flops | bytes accessed | tf_op | source)
XLA Modules:
  0.0 183.3 jit_solution(15130381761060317966)
XLA Ops:
  0.0 1.9 %slice.60 = bf16[6,64,768]{2,1,0:T(8,128)(2,1)} slice(bf16[6,256,768]{2,1,0:T(8,128)(2,1)} %factors_ref.9), slice={[0:6], [0:64], [0:768]} | slice | bytes 1179648 | tf_op jit(solution)/shard_map/slice | solution.py:356
  1.9 4.1 %collective-permute-start = (bf16[6,64,768]{2,1,0:T(8,128)(2,1)}, bf16[6,64,768]{2,1,0:T(8,128)(2,1)}, u32[]{:S(2)}, u32[]{:S(2)}) collective-permute-start(bf16[6,64,768]{2,1,0:T(8,128)(2,1)} %slice.60), channel_id=1, source_target_pairs={{0,16},{4,20},{8,24},{12,28},{16,0},{20,4},{24,8},{28,12},{1,17},{... | collective-permute-start | bytes 1769480 | tf_op jit(solution)/shard_map/ppermute | solution.py:19
  6.0 2.1 %slice.61 = bf16[6,96,768]{2,1,0:T(8,128)(2,1)} slice(bf16[6,256,768]{2,1,0:T(8,128)(2,1)} %factors_ref.9), slice={[0:6], [64:160], [0:768]} | slice | bytes 1769472 | tf_op jit(solution)/shard_map/slice | solution.py:358
  8.2 3.9 %take_near.1 = (bf16[2,256,768]{2,1,0:T(8,128)(2,1)}, bf16[2,256,768]{2,1,0:T(8,128)(2,1)}, bf16[2,256,768]{2,1,0:T(8,128)(2,1)}) custom-call(s32[4,192]{1,0:T(4,128)} %bitcast.144, bf16[6,256,768]{2,1,0:T(8,128)(2,1)} %factors_ref.9), custom_call_target="tpu_custom_call" | custom-call | bytes 4718592 | tf_op jit(solution)/shard_map/take_near/pallas_call | solution.py:67
  12.1 1.9 %collective-permute-start.12 = (bf16[2,256,768]{2,1,0:T(8,128)(2,1)}, bf16[2,256,768]{2,1,0:T(8,128)(2,1)}, u32[]{:S(2)}, u32[]{:S(2)}) collective-permute-start(bf16[2,256,768]{2,1,0:T(8,128)(2,1)} %get-tuple-element.54), channel_id=1, source_target_pairs={{0,4},{4,0},{8,12},{12,8},{16,20},{20,16},{24,28},{28,24},{1,5},{5... | collective-permute-start | bytes 2359304 | tf_op jit(solution)/shard_map/ppermute | solution.py:19
  18.0 34.2 %collective-permute-done.source_ref.refs_0_ = bf16[6,64,768]{2,1,0:T(8,128)(2,1)} collective-permute-done((bf16[6,64,768]{2,1,0:T(8,128)(2,1)}, bf16[6,64,768]{2,1,0:T(8,128)(2,1)}, u32[]{:S(2)}, u32[]{:S(2)}) %collective-permute-start) | collective-permute-done | bytes 589856 | tf_op jit(solution)/shard_map/ppermute | solution.py:19
  52.2 2.4 %take_pairs.3 = (bf16[2,64,768]{2,1,0:T(8,128)(2,1)}, bf16[2,64,768]{2,1,0:T(8,128)(2,1)S(1)}, bf16[2,64,768]{2,1,0:T(8,128)(2,1)S(1)}) custom-call(s32[32]{0:T(128)S(1)} %reshape.348.index_ref, bf16[6,64,768]{2,1,0:T(8,128)(2,1)} %collective-permute-done.source_ref.refs_0_), custom_call_target="tpu_custom_call" | custom-call | bytes 1179648 | tf_op jit(solution)/shard_map/take_pairs/pallas_call | solution.py:87
  55.3 28.7 %collective-permute-done.5.refs_0_ = bf16[2,64,768]{2,1,0:T(8,128)(2,1)S(1)} collective-permute-done((bf16[2,64,768]{2,1,0:T(8,128)(2,1)S(1)}, bf16[2,64,768]{2,1,0:T(8,128)(2,1)S(1)}, u32[]{:S(2)}, u32[]{:S(2)}) %collective-permute-start.5) | collective-permute-done | bytes 196640 | tf_op jit(solution)/shard_map/ppermute | solution.py:19
  87.2 3.0 %take_pairs.5 = (bf16[2,96,768]{2,1,0:T(8,128)(2,1)}, bf16[2,96,768]{2,1,0:T(8,128)(2,1)}, bf16[2,96,768]{2,1,0:T(8,128)(2,1)S(1)}, bf16[2,96,768]{2,1,0:T(8,128)(2,1)S(1)}) custom-call(s32[32]{0:T(128)S(1)} %reshape.348.index_ref, bf16[6,256,768]{2,1,0:T(8,128)(2,1)S(1)} %copy-done), custom_call_target="tpu_custom_call" | custom-call | bytes 2359296 | tf_op jit(solution)/shard_map/take_pairs/pallas_call | solution.py:87
  90.6 2.5 %collective-permute-start.8 = (bf16[2,96,768]{2,1,0:T(8,128)(2,1)}, bf16[2,96,768]{2,1,0:T(8,128)(2,1)}, u32[]{:S(2)}, u32[]{:S(2)}) collective-permute-start(bf16[2,96,768]{2,1,0:T(8,128)(2,1)} %get-tuple-element.50), channel_id=1, source_target_pairs={{0,16},{4,20},{8,24},{12,28},{16,0},{20,4},{24,8},{28,12},{1,17},{... | collective-permute-start | bytes 884744 | tf_op jit(solution)/shard_map/ppermute | solution.py:19
  95.9 2.5 %take_pairs.4 = (bf16[2,96,768]{2,1,0:T(8,128)(2,1)}, bf16[2,96,768]{2,1,0:T(8,128)(2,1)S(1)}, bf16[2,96,768]{2,1,0:T(8,128)(2,1)S(1)}) custom-call(s32[32]{0:T(128)S(1)} %reshape.348.index_ref, bf16[6,96,768]{2,1,0:T(8,128)(2,1)S(1)} %collective-permute-done.2.source_ref.refs_1_), custom_call_target="tpu_custom_call" | custom-call | bytes 1769472 | tf_op jit(solution)/shard_map/take_pairs/pallas_call | solution.py:87
  102.2 4.5 %collective-permute-start.7 = (bf16[2,96,768]{2,1,0:T(8,128)(2,1)}, bf16[2,96,768]{2,1,0:T(8,128)(2,1)S(1)}, u32[]{:S(2)}, u32[]{:S(2)}) collective-permute-start(bf16[2,96,768]{2,1,0:T(8,128)(2,1)} %copy-done.7), channel_id=1, source_target_pairs={{0,24},{4,28},{8,16},{12,20},{16,8},{20,12},{24,0},{28,4},{1,25},{... | collective-permute-start | bytes 884744 | tf_op jit(solution)/shard_map/ppermute | solution.py:19
  106.7 3.3 %pair_terms.4.refs_3_ = f32[6,256,768]{2,1,0:T(8,128)S(1)} custom-call(s32[88]{0:T(128)S(1)} %reshape.346.meta_ref, f32[8,8,256]{2,1,0:T(8,128)S(1)} %bitcast.129, bf16[6,256,768]{2,1,0:T(8,128)(2,1)S(1)} %copy-done.1, bf16[6,256,768]{2,1,0:T(8,128)(2,1)S(1)} %copy-done.1), custom_call_target="tpu_custom_call" | custom-call | flops 603979776 | bytes 786432 | tf_op jit(solution)/shard_map/pair_terms/pallas_call | solution.py:180
  110.0 9.5 %collective-permute-done.8.refs_2_ = bf16[2,96,768]{2,1,0:T(8,128)(2,1)} collective-permute-done((bf16[2,96,768]{2,1,0:T(8,128)(2,1)}, bf16[2,96,768]{2,1,0:T(8,128)(2,1)}, u32[]{:S(2)}, u32[]{:S(2)}) %collective-permute-start.8) | collective-permute-done | bytes 294944 | tf_op jit(solution)/shard_map/ppermute | solution.py:19
  121.2 11.1 %collective-permute-done.11.refs_5_ = bf16[2,96,768]{2,1,0:T(8,128)(2,1)} collective-permute-done((bf16[2,96,768]{2,1,0:T(8,128)(2,1)}, bf16[2,96,768]{2,1,0:T(8,128)(2,1)}, u32[]{:S(2)}, u32[]{:S(2)}) %collective-permute-start.11) | collective-permute-done | bytes 294944 | tf_op jit(solution)/shard_map/ppermute | solution.py:19
  132.3 7.8 %pair_terms.5.refs_6_ = f32[6,256,768]{2,1,0:T(8,128)S(1)} custom-call(s32[88]{0:T(128)S(1)} %reshape.346.meta_ref, f32[8,8,256]{2,1,0:T(8,128)S(1)} %bitcast.130, bf16[6,256,768]{2,1,0:T(8,128)(2,1)S(1)} %copy-done.1, bf16[2,256,768]{2,1,0:T(8,128)(2,1)} %collective-permute-done.12.refs_0_, ...), custom_call_target="tpu_custom_call", output_to_operand_aliasing={{}: (6, {})} | custom-call | flops 1811939328 | bytes 2359296 | tf_op jit(solution)/shard_map/pair_terms/pallas_call | solution.py:180
  140.2 3.0 %collective-permute-start.1 = (bf16[2,64,768]{2,1,0:T(8,128)(2,1)S(1)}, bf16[2,64,768]{2,1,0:T(8,128)(2,1)S(1)}, u32[]{:S(2)}, u32[]{:S(2)}) collective-permute-start(bf16[2,64,768]{2,1,0:T(8,128)(2,1)S(1)} %copy-done.12), channel_id=1, source_target_pairs={{0,12},{4,8},{8,4},{12,0},{16,28},{20,24},{24,20},{28,16},{1,13},{... | collective-permute-start | bytes 589832 | tf_op jit(solution)/shard_map/ppermute | solution.py:19
  143.1 6.3 %pair_terms.6.refs_3_ = f32[6,256,768]{2,1,0:T(8,128)S(1)} custom-call(s32[88]{0:T(128)S(1)} %reshape.346.meta_ref, f32[8,8,256]{2,1,0:T(8,128)S(1)} %bitcast.131, bf16[6,256,768]{2,1,0:T(8,128)(2,1)S(1)} %copy-done.1, bf16[6,64,768]{2,1,0:T(8,128)(2,1)} %collective-permute-done.source_ref.refs_0_, ...), custom_call_target="tpu_custom_call", output_to_operand_aliasing={{}: (9, {})} | custom-call | flops 1207959552 | bytes 1572864 | tf_op jit(solution)/shard_map/pair_terms/pallas_call | solution.py:180
  149.5 3.7 %pair_terms.7.density_ref.refs_3_ = f32[6,256,768]{2,1,0:T(8,128)S(1)} custom-call(s32[88]{0:T(128)S(1)} %reshape.346.meta_ref, f32[8,8,256]{2,1,0:T(8,128)S(1)} %bitcast.132, bf16[6,256,768]{2,1,0:T(8,128)(2,1)S(1)} %copy-done.1, bf16[2,64,768]{2,1,0:T(8,128)(2,1)S(1)} %copy-done.4, ...), custom_call_target="tpu_custom_call", output_to_operand_aliasing={{}: (6, {})} | custom-call | flops 603979776 | bytes 786432 | tf_op jit(solution)/shard_map/pair_terms/pallas_call | solution.py:180
  153.2 2.3 %partial_total.1.refs_5_ = f32[768,768]{1,0:T(8,128)S(1)} custom-call(s32[88]{0:T(128)S(1)} %reshape.346.meta_ref, bf16[6,256,768]{2,1,0:T(8,128)(2,1)S(1)} %copy-done.2, f32[6,256,768]{2,1,0:T(8,128)S(1)} %pair_terms.7.density_ref.refs_3_), custom_call_target="tpu_custom_call" | custom-call | flops 905969664 | bytes 1179648 | tf_op jit(solution)/shard_map/partial_total/pallas_call | solution.py:224
  155.5 5.6 %finish.1 = (f32[2,8,144,128]{3,2,1,0:T(8,128)S(1)}, bf16[2,8,144,128]{3,2,1,0:T(8,128)(2,1)S(1)}, f32[6,256,768]{2,1,0:T(8,128)S(1)}, f32[768,768]{1,0:T(8,128)S(1)}) custom-call(s32[88]{0:T(128)S(1)} %reshape.346.meta_ref, s32[1]{0:T(128)} %bitcast.13.parity_ref, f32[8,8,256]{2,1,0:T(8,128)S(1)} %bitcast.133, ...), custom_call_target="tpu_custom_call", output_to_operand_aliasing={{2}: (7, {}), {3}: (9, {})} | custom-call | flops 1811939328 | bytes 7077888 | tf_op jit(solution)/shard_map/finish/pallas_call | solution.py:309
  161.2 2.0 %collective-permute-done.15 = bf16[2,8,144,128]{3,2,1,0:T(8,128)(2,1)S(1)} collective-permute-done((bf16[2,8,144,128]{3,2,1,0:T(8,128)(2,1)S(1)}, bf16[2,8,144,128]{3,2,1,0:T(8,128)(2,1)S(1)}, u32[]{:S(2)}, u32[]{:S(2)}) %collective-permute-start.15) | collective-permute-done | bytes 589856 | tf_op jit(solution)/shard_map/ppermute | solution.py:19
  166.3 3.1 %collective-permute-done.16 = bf16[1,4,144,128]{3,2,1,0:T(8,128)(2,1)S(1)} collective-permute-done((bf16[1,4,144,128]{3,2,1,0:T(8,128)(2,1)S(1)}, bf16[1,4,144,128]{3,2,1,0:T(8,128)(2,1)S(1)}, u32[]{:S(2)}, u32[]{:S(2)}) %collective-permute-start.16) | collective-permute-done | bytes 147488 | tf_op jit(solution)/shard_map/ppermute | solution.py:19
  177.5 2.5 %collective-permute-start.21 = (bf16[144,128]{1,0:T(8,128)(2,1)S(1)}, bf16[144,128]{1,0:T(8,128)(2,1)S(1)}, u32[]{:S(2)}, u32[]{:S(2)}) collective-permute-start(bf16[144,128]{1,0:T(8,128)(2,1)S(1)} %get-tuple-element.76), channel_id=1, source_target_pairs={{0,16},{4,20},{8,24},{12,28},{16,0},{20,4},{24,8},{28,12},{1,17},{... | collective-permute-start | bytes 110600 | tf_op jit(solution)/shard_map/ppermute | solution.py:19
  (122 shorter events, 31.0 us)
Async XLA Ops:
  1.9 50.3 %collective-permute-start = (bf16[6,64,768]{2,1,0:T(8,128)(2,1)}, bf16[6,64,768]{2,1,0:T(8,128)(2,1)}, u32[]{:S(2)}, u32[]{:S(2)}) collective-permute-start(bf16[6,64,768]{2,1,0:T(8,128)(2,1)} %slice.60), channel_id=1, source_target_pairs={{0,16},{4,20},{8,24},{12,28},{16,0},{20,4},{24,8},{28,12},{1,17},{... | collective-permute-start | bytes 1769480 | tf_op jit(solution)/shard_map/ppermute | solution.py:19
  8.1 84.9 %collective-permute-start.2 = (bf16[6,96,768]{2,1,0:T(8,128)(2,1)}, bf16[6,96,768]{2,1,0:T(8,128)(2,1)S(1)}, u32[]{:S(2)}, u32[]{:S(2)}) collective-permute-start(bf16[6,96,768]{2,1,0:T(8,128)(2,1)} %slice.61), channel_id=1, source_target_pairs={{0,16},{4,20},{8,24},{12,28},{16,0},{20,4},{24,8},{28,12},{1,17},{... | collective-permute-start | bytes 2654216 | tf_op jit(solution)/shard_map/ppermute | solution.py:19
  12.0 82.2 %copy-start.14 = (f32[192]{0:T(256)S(1)}, f32[192]{0:T(256)}, u32[]{:S(2)}) copy-start(f32[192]{0:T(256)} %param.8) | copy-start | bytes 2308
  12.1 87.8 %collective-permute-start.12 = (bf16[2,256,768]{2,1,0:T(8,128)(2,1)}, bf16[2,256,768]{2,1,0:T(8,128)(2,1)}, u32[]{:S(2)}, u32[]{:S(2)}) collective-permute-start(bf16[2,256,768]{2,1,0:T(8,128)(2,1)} %get-tuple-element.54), channel_id=1, source_target_pairs={{0,4},{4,0},{8,12},{12,8},{16,20},{20,16},{24,28},{28,24},{1,5},{5... | collective-permute-start | bytes 2359304 | tf_op jit(solution)/shard_map/ppermute | solution.py:19
  14.0 88.2 %collective-permute-start.13 = (bf16[2,256,768]{2,1,0:T(8,128)(2,1)}, bf16[2,256,768]{2,1,0:T(8,128)(2,1)}, u32[]{:S(2)}, u32[]{:S(2)}) collective-permute-start(bf16[2,256,768]{2,1,0:T(8,128)(2,1)} %get-tuple-element.55), channel_id=1, source_target_pairs={{0,8},{4,12},{8,0},{12,4},{16,24},{20,28},{24,16},{28,20},{1,9},{5... | collective-permute-start | bytes 2359304 | tf_op jit(solution)/shard_map/ppermute | solution.py:19
  15.0 91.6 %collective-permute-start.14 = (bf16[2,256,768]{2,1,0:T(8,128)(2,1)}, bf16[2,256,768]{2,1,0:T(8,128)(2,1)}, u32[]{:S(2)}, u32[]{:S(2)}) collective-permute-start(bf16[2,256,768]{2,1,0:T(8,128)(2,1)} %get-tuple-element.56), channel_id=1, source_target_pairs={{0,12},{4,8},{8,4},{12,0},{16,28},{20,24},{24,20},{28,16},{1,13},{... | collective-permute-start | bytes 2359304 | tf_op jit(solution)/shard_map/ppermute | solution.py:19
  55.3 28.7 %collective-permute-start.5 = (bf16[2,64,768]{2,1,0:T(8,128)(2,1)S(1)}, bf16[2,64,768]{2,1,0:T(8,128)(2,1)S(1)}, u32[]{:S(2)}, u32[]{:S(2)}) collective-permute-start(bf16[2,64,768]{2,1,0:T(8,128)(2,1)S(1)} %get-tuple-element.47), channel_id=1, source_target_pairs={{0,8},{4,12},{8,0},{12,4},{16,24},{20,28},{24,16},{28,20},{1,9},{5... | collective-permute-start | bytes 589832 | tf_op jit(solution)/shard_map/ppermute | solution.py:19
  84.7 5.9 %collective-permute-start.9 = (bf16[2,64,768]{2,1,0:T(8,128)(2,1)}, bf16[2,64,768]{2,1,0:T(8,128)(2,1)S(1)}, u32[]{:S(2)}, u32[]{:S(2)}) collective-permute-start(bf16[2,64,768]{2,1,0:T(8,128)(2,1)} %get-tuple-element.51), channel_id=1, source_target_pairs={{0,4},{4,0},{8,12},{12,8},{16,20},{20,16},{24,28},{28,24},{1,5},{5... | collective-permute-start | bytes 589832 | tf_op jit(solution)/shard_map/ppermute | solution.py:19
  90.6 28.9 %collective-permute-start.8 = (bf16[2,96,768]{2,1,0:T(8,128)(2,1)}, bf16[2,96,768]{2,1,0:T(8,128)(2,1)}, u32[]{:S(2)}, u32[]{:S(2)}) collective-permute-start(bf16[2,96,768]{2,1,0:T(8,128)(2,1)} %get-tuple-element.50), channel_id=1, source_target_pairs={{0,16},{4,20},{8,24},{12,28},{16,0},{20,4},{24,8},{28,12},{1,17},{... | collective-permute-start | bytes 884744 | tf_op jit(solution)/shard_map/ppermute | solution.py:19
  93.1 39.2 %collective-permute-start.11 = (bf16[2,96,768]{2,1,0:T(8,128)(2,1)}, bf16[2,96,768]{2,1,0:T(8,128)(2,1)}, u32[]{:S(2)}, u32[]{:S(2)}) collective-permute-start(bf16[2,96,768]{2,1,0:T(8,128)(2,1)} %get-tuple-element.53), channel_id=1, source_target_pairs={{0,20},{4,16},{8,28},{12,24},{16,4},{20,0},{24,12},{28,8},{1,21},{... | collective-permute-start | bytes 884744 | tf_op jit(solution)/shard_map/ppermute | solution.py:19
  99.8 40.3 %collective-permute-start.10 = (bf16[2,96,768]{2,1,0:T(8,128)(2,1)}, bf16[2,96,768]{2,1,0:T(8,128)(2,1)}, u32[]{:S(2)}, u32[]{:S(2)}) collective-permute-start(bf16[2,96,768]{2,1,0:T(8,128)(2,1)} %get-tuple-element.52), channel_id=1, source_target_pairs={{0,4},{4,0},{8,12},{12,8},{16,20},{20,16},{24,28},{28,24},{1,5},{5... | collective-permute-start | bytes 884744 | tf_op jit(solution)/shard_map/ppermute | solution.py:19
  102.2 47.3 %collective-permute-start.7 = (bf16[2,96,768]{2,1,0:T(8,128)(2,1)}, bf16[2,96,768]{2,1,0:T(8,128)(2,1)S(1)}, u32[]{:S(2)}, u32[]{:S(2)}) collective-permute-start(bf16[2,96,768]{2,1,0:T(8,128)(2,1)} %copy-done.7), channel_id=1, source_target_pairs={{0,24},{4,28},{8,16},{12,20},{16,8},{20,12},{24,0},{28,4},{1,25},{... | collective-permute-start | bytes 884744 | tf_op jit(solution)/shard_map/ppermute | solution.py:19
  106.7 42.8 %collective-permute-start.6 = (bf16[2,96,768]{2,1,0:T(8,128)(2,1)}, bf16[2,96,768]{2,1,0:T(8,128)(2,1)S(1)}, u32[]{:S(2)}, u32[]{:S(2)}) collective-permute-start(bf16[2,96,768]{2,1,0:T(8,128)(2,1)} %copy-done.10), channel_id=1, source_target_pairs={{0,8},{4,12},{8,0},{12,4},{16,24},{20,28},{24,16},{28,20},{1,9},{5... | collective-permute-start | bytes 884744 | tf_op jit(solution)/shard_map/ppermute | solution.py:19
  119.5 36.0 %collective-permute-start.4 = (bf16[2,96,768]{2,1,0:T(8,128)(2,1)S(1)}, bf16[2,96,768]{2,1,0:T(8,128)(2,1)S(1)}, u32[]{:S(2)}, u32[]{:S(2)}) collective-permute-start(bf16[2,96,768]{2,1,0:T(8,128)(2,1)S(1)} %copy-done.6), channel_id=1, source_target_pairs={{0,28},{4,24},{8,20},{12,16},{16,12},{20,8},{24,4},{28,0},{1,29},{... | collective-permute-start | bytes 884744 | tf_op jit(solution)/shard_map/ppermute | solution.py:19
  132.3 23.2 %collective-permute-start.3 = (bf16[2,96,768]{2,1,0:T(8,128)(2,1)S(1)}, bf16[2,96,768]{2,1,0:T(8,128)(2,1)S(1)}, u32[]{:S(2)}, u32[]{:S(2)}) collective-permute-start(bf16[2,96,768]{2,1,0:T(8,128)(2,1)S(1)} %copy-done.9), channel_id=1, source_target_pairs={{0,12},{4,8},{8,4},{12,0},{16,28},{20,24},{24,20},{28,16},{1,13},{... | collective-permute-start | bytes 884744 | tf_op jit(solution)/shard_map/ppermute | solution.py:19
  140.2 15.3 %collective-permute-start.1 = (bf16[2,64,768]{2,1,0:T(8,128)(2,1)S(1)}, bf16[2,64,768]{2,1,0:T(8,128)(2,1)S(1)}, u32[]{:S(2)}, u32[]{:S(2)}) collective-permute-start(bf16[2,64,768]{2,1,0:T(8,128)(2,1)S(1)} %copy-done.12), channel_id=1, source_target_pairs={{0,12},{4,8},{8,4},{12,0},{16,28},{20,24},{24,20},{28,16},{1,13},{... | collective-permute-start | bytes 589832 | tf_op jit(solution)/shard_map/ppermute | solution.py:19
  161.1 2.1 %collective-permute-start.15 = (bf16[2,8,144,128]{3,2,1,0:T(8,128)(2,1)S(1)}, bf16[2,8,144,128]{3,2,1,0:T(8,128)(2,1)S(1)}, u32[]{:S(2)}, u32[]{:S(2)}) collective-permute-start(bf16[2,8,144,128]{3,2,1,0:T(8,128)(2,1)S(1)} %get-tuple-element.58), channel_id=1, source_target_pairs={{0,1},{1,0},{2,3},{3,2},{4,5},{5,4},{6,7},{7,6},{8,9},{9,8},{10,11... | collective-permute-start | bytes 1769480 | tf_op jit(solution)/shard_map/ppermute | solution.py:19
  163.4 6.0 %collective-permute-start.16 = (bf16[1,4,144,128]{3,2,1,0:T(8,128)(2,1)S(1)}, bf16[1,4,144,128]{3,2,1,0:T(8,128)(2,1)S(1)}, u32[]{:S(2)}, u32[]{:S(2)}) collective-permute-start(bf16[1,4,144,128]{3,2,1,0:T(8,128)(2,1)S(1)} %fusion.4), channel_id=1, source_target_pairs={{0,2},{1,3},{2,0},{3,1},{4,6},{5,7},{6,4},{7,5},{8,10},{9,11},{10,... | collective-permute-start | bytes 442376 | tf_op jit(solution)/shard_map/ppermute | solution.py:19
  165.3 5.7 %collective-permute-start.18 = (bf16[2,2,144,128]{3,2,1,0:T(8,128)(2,1)S(1)}, bf16[2,2,144,128]{3,2,1,0:T(8,128)(2,1)S(1)}, u32[]{:S(2)}, u32[]{:S(2)}) collective-permute-start(bf16[2,2,144,128]{3,2,1,0:T(8,128)(2,1)S(1)} %fusion.5), channel_id=1, source_target_pairs={{0,4},{4,0},{8,12},{12,8},{16,20},{20,16},{24,28},{28,24},{1,5},{5... | collective-permute-start | bytes 442376 | tf_op jit(solution)/shard_map/ppermute | solution.py:19
  169.5 4.4 %collective-permute-start.17 = (bf16[1,2,144,128]{3,2,1,0:T(8,128)(2,1)S(1)}, bf16[1,2,144,128]{3,2,1,0:T(8,128)(2,1)S(1)}, u32[]{:S(2)}, u32[]{:S(2)}) collective-permute-start(bf16[1,2,144,128]{3,2,1,0:T(8,128)(2,1)S(1)} %fusion.6), channel_id=1, source_target_pairs={{0,4},{4,0},{8,12},{12,8},{16,20},{20,16},{24,28},{28,24},{1,5},{5... | collective-permute-start | bytes 221192 | tf_op jit(solution)/shard_map/ppermute | solution.py:19
  171.0 4.4 %collective-permute-start.19 = (bf16[1,2,144,128]{3,2,1,0:T(8,128)(2,1)S(1)}, bf16[1,2,144,128]{3,2,1,0:T(8,128)(2,1)S(1)}, u32[]{:S(2)}, u32[]{:S(2)}) collective-permute-start(bf16[1,2,144,128]{3,2,1,0:T(8,128)(2,1)S(1)} %fusion.7), channel_id=1, source_target_pairs={{0,2},{1,3},{2,0},{3,1},{4,6},{5,7},{6,4},{7,5},{8,10},{9,11},{10,... | collective-permute-start | bytes 221192 | tf_op jit(solution)/shard_map/ppermute | solution.py:19
  175.6 5.9 %collective-permute-start.20 = (bf16[144,128]{1,0:T(8,128)(2,1)S(1)}, bf16[144,128]{1,0:T(8,128)(2,1)S(1)}, u32[]{:S(2)}, u32[]{:S(2)}) collective-permute-start(bf16[144,128]{1,0:T(8,128)(2,1)S(1)} %get-tuple-element.74), channel_id=1, source_target_pairs={{0,24},{4,28},{8,16},{12,20},{16,8},{20,12},{24,0},{28,4},{1,25},{... | collective-permute-start | bytes 110600 | tf_op jit(solution)/shard_map/ppermute | solution.py:19
  177.5 4.3 %collective-permute-start.22 = (bf16[144,128]{1,0:T(8,128)(2,1)S(1)}, bf16[144,128]{1,0:T(8,128)(2,1)S(1)}, u32[]{:S(2)}, u32[]{:S(2)}) collective-permute-start(bf16[144,128]{1,0:T(8,128)(2,1)S(1)} %get-tuple-element.75), channel_id=1, source_target_pairs={{0,8},{4,12},{8,0},{12,4},{16,24},{20,28},{24,16},{28,20},{1,9},{5... | collective-permute-start | bytes 110600 | tf_op jit(solution)/shard_map/ppermute | solution.py:19
  177.5 4.9 %collective-permute-start.21 = (bf16[144,128]{1,0:T(8,128)(2,1)S(1)}, bf16[144,128]{1,0:T(8,128)(2,1)S(1)}, u32[]{:S(2)}, u32[]{:S(2)}) collective-permute-start(bf16[144,128]{1,0:T(8,128)(2,1)S(1)} %get-tuple-element.76), channel_id=1, source_target_pairs={{0,16},{4,20},{8,24},{12,28},{16,0},{20,4},{24,8},{28,12},{1,17},{... | collective-permute-start | bytes 110600 | tf_op jit(solution)/shard_map/ppermute | solution.py:19
  (14 other events, 117.7 us)
